TPU v7x, 256 devices: a whole 4x4x8 slice. The times are simulated.
256 devices in a mesh: row: 16 (over z_lo, x, core), col: 16 (over y, z_hi).
Axes of the slice: x: 4, y: 4, z: 8 (z_hi: 4, z_lo: 2; z = z_hi * 2 + z_lo), core: 2. Of those that a mesh axis runs over, the one named last changes fastest.
Arguments:
- pair: bfloat16 [768, 768, 128], P('row', 'col'), may hold values from -6 to 6
- ln_gain: float32 [128], replicated, may hold values from 0.25 to 1.75
- w_query: bfloat16 [128, 128], replicated, may hold values from -46 to 46
- w_key: bfloat16 [128, 128], replicated, may hold values from -0.5 to 0.5
- w_value: bfloat16 [128, 128], replicated, may hold values from -0.5 to 0.5
- w_gate: bfloat16 [128, 128], replicated, may hold values from -0.5 to 0.5
- w_bias: bfloat16 [128, 4], replicated, may hold values from -0.5 to 0.5
- w_out: bfloat16 [128, 128], replicated, may hold values from -0.5 to 0.5
- valid_length: int32 [1], replicated, may hold values from 384 to 768
Outputs:
- update: bfloat16 [768, 768, 128], P('row', 'col')
Inputs may be any that keep to these rules, and one draw needn't show every extreme that they name: Tokens 0 to valid_length - 1 are real, the others are padding.
All inputs are finite; a program needn't handle non-finite values.
Results may differ from a plain program's by a relative error of at most 0.014.
The roundings to bfloat16 on the way count: a program that leaves them out, or rounds other values in their place, can miss the bound.
Values may be sent and summed in bfloat16 or wider, within the bound.
No kernel may reach another device: no remote copies, remote signals or barrier semaphores. Data moves between devices by JAX's collectives and lax.ppermute only.
A program may use at most 128 MiB of HBM per device.

v0:
```python
import jax
import jax.numpy as jnp
from jax import lax
from jax.sharding import PartitionSpec as P

epsilon = 1e-05


def cut_along(value, dim, length):
    before, after = (value.shape[:dim], value.shape[dim + 1 :])
    return jnp.moveaxis(value.reshape(*before, length, -1, *after), dim, 0)


def edges_of(length, count):
    lap = length // count
    if lap >= 8:
        lap -= lap % 8
    return [lap * k for k in range(1, count)]


def in_order(blocks, dim):
    lengths = list(blocks.shape[1:])
    lengths[dim] *= blocks.shape[0]
    return jnp.moveaxis(blocks, 0, dim).reshape(lengths)


def several_exchanges(value, axis, pieces, split_dim, concat_dim):
    blocks = cut_along(value, split_dim, lax.axis_size(axis))
    widest = max(range(1, max(2, blocks.ndim - 1)), key=lambda d: blocks.shape[d])
    outs = []
    for slab in jnp.split(blocks, edges_of(blocks.shape[widest], pieces), axis=widest):
        if slab.size:
            outs.append(lax.all_to_all(slab, axis, split_axis=0, concat_axis=0, tiled=True))
    return in_order(jnp.concatenate(outs, axis=widest), concat_dim)


def from_everyone(value, axis):
    length = lax.axis_size(axis)
    return lax.all_to_all(
        jnp.broadcast_to(value[None], (length, *value.shape)), axis, 0, 0, tiled=True
    )


def collect(value, axis, dim):
    return in_order(from_everyone(value, axis), dim)


def normalize(pair_rows, ln_gain):
    widened = pair_rows.astype(jnp.float32)
    average = jnp.mean(widened, -1, keepdims=True)
    centred = widened - average
    spread = jnp.mean(centred * centred, -1, keepdims=True)
    return (centred * lax.rsqrt(spread + epsilon) * ln_gain).astype(jnp.bfloat16)


def per_device(pair, ln_gain, w_query, w_key, w_value, w_gate, w_bias, w_out, valid_length):
    tile_rows, tile_cols, channels = pair.shape
    heads = w_bias.shape[1]
    width = w_query.shape[1]
    head_size = width // heads
    across = lax.axis_size("col")
    own_rows = tile_rows // across
    columns = tile_cols * across
    query_scale = head_size ** (-0.5)
    length = valid_length[0]
    normed = normalize(pair, ln_gain)
    bias_tile = jnp.einsum(
        "abc,ch->hab", normed, w_bias, preferred_element_type=jnp.float32
    ).astype(jnp.bfloat16)
    merged = jnp.concatenate([w_query, w_key, w_value, w_gate], axis=1)
    normed_rows = several_exchanges(normed, "col", 2, 0, 1)
    target_shape = normed_rows.shape[:2] + (width,)
    flattened = normed_rows.reshape(-1, channels)
    projected = jnp.dot(flattened, merged, preferred_element_type=jnp.float32)
    query = (projected[:, :width] * query_scale).astype(jnp.bfloat16).reshape(target_shape)
    key_proj = projected[:, width : 2 * width].astype(jnp.bfloat16).reshape(target_shape)
    value_proj = projected[:, 2 * width : 3 * width].astype(jnp.bfloat16).reshape(target_shape)
    project_gating = (
        jax.nn.sigmoid(projected[:, 3 * width :]).astype(jnp.bfloat16).reshape(target_shape)
    )
    query, key_proj, value_proj, gating = (query, key_proj, value_proj, project_gating)
    query_heads = query.reshape(own_rows, columns, heads, head_size)
    key_heads = key_proj.reshape(own_rows, columns, heads, head_size)
    value_heads = value_proj.reshape(own_rows, columns, heads, head_size)
    positions = jnp.arange(columns, dtype=jnp.int32)
    key_valid = positions < length
    first_row = lax.axis_index("row") * tile_rows + lax.axis_index("col") * own_rows
    row_valid = first_row + jnp.arange(own_rows, dtype=jnp.int32) < length
    bias_cols = collect(bias_tile, "col", 2)
    portion = lax.all_gather(bias_cols, "row", axis=1, tiled=True)
    extent = portion.shape[1]
    scores = jnp.einsum(
        "ijhd,ikhd->ihjk", query_heads, key_heads, preferred_element_type=jnp.float32
    )
    scores = scores + portion.astype(jnp.float32)[None]
    scores = jnp.where(key_valid, scores, -1e30)
    highest = jnp.max(scores, -1, keepdims=True)
    exponent = jnp.exp(scores - highest)
    totals = jnp.sum(exponent, -1)
    weights = exponent.astype(jnp.bfloat16)
    blended = jnp.einsum(
        "ihjk,ikhd->ijhd", weights, value_heads, preferred_element_type=jnp.float32
    )
    blended = blended / jnp.transpose(totals, (0, 2, 1))[..., None]
    gated = (gating.astype(jnp.float32) * blended.reshape(own_rows, extent, width)).astype(
        jnp.bfloat16
    )
    update = jnp.dot(gated.reshape(-1, width), w_out, preferred_element_type=jnp.float32).reshape(
        own_rows, columns, channels
    )
    inside = row_valid[:, None] & key_valid[None, :]
    update = jnp.where(inside[..., None], update, 0.0).astype(jnp.bfloat16)
    return lax.all_to_all(update, "col", split_axis=1, concat_axis=0, tiled=True)


def solution(mesh):
    placed = (P("row", "col", None), P(), P(), P(), P(), P(), P(), P(), P())
    return jax.shard_map(
        per_device, mesh=mesh, in_specs=placed, out_specs=P("row", "col", None), check_vma=False
    )
```

profile of v0, /device:TPU:2, one launch (start us, length us, event | category | flops | bytes accessed | tf_op | source)
XLA Modules:
  0.0 190.3 jit_solution(926397848877025164)
XLA Ops:
  6.5 0.0 copy-start
  6.5 0.0 all-gather.2.cloned.1.call-start
  6.5 1.4 convert_reduce_fusion
  8.0 1.8 fusion.15
  9.8 1.7 fusion.17
  11.5 1.3 fusion.23
  12.9 0.1 copy.76
  13.0 0.1 broadcast_bitcast_fusion
  13.2 1.2 reshape.73
  14.3 25.0 %all_to_all.33 = bf16[16,2,4608]{2,1,0:T(2,128)(2,1)S(1)} all-to-all(bf16[16,2,4608]{2,1,0:T(2,128)(2,1)S(1)} %reshape.73), channel_id=1, replica_groups=mesh['row'=16,'col'=16] {'col'}, dimensions={0} | all-to-all | bytes 589824 | tf_op jit(solution)/shard_map/all_to_all | solution.py:39
  39.3 0.8 reshape.74
  40.1 0.0 copy-start.2
  40.1 0.0 copy-start.3
  40.1 0.0 copy-start.4
  40.1 0.0 copy-start.5
  40.1 0.1 bitcast_bitcast_fusion
  40.2 1.3 copy.88
  41.5 1.6 reshape.72
  43.1 0.0 all-gather.2.cloned.1.call-update
  43.1 0.8 fusion.41
  43.9 15.9 %all_to_all.34 = bf16[16,3,24,128]{3,2,1,0:T(8,128)(2,1)S(1)} all-to-all(bf16[16,3,24,128]{3,2,1,0:T(8,128)(2,1)S(1)} %get-tuple-element.7), channel_id=1, replica_groups=mesh['row'=16,'col'=16] {'col'}, dimensions={0} | all-to-all | bytes 589824 | tf_op jit(solution)/shard_map/all_to_all | solution.py:33
  59.8 3.7 %all-to-all-start.1 = ((bf16[16,3,24,128]{3,2,1,0:T(8,128)(2,1)}), bf16[16,3,24,128]{3,2,1,0:T(8,128)(2,1)S(1)}, u32[]{:S(2)}, u32[]{:S(2)}) async-start(bf16[16,3,24,128]{3,2,1,0:T(8,128)(2,1)} %get-tuple-element.8), calls=%async_computation.1 | async-start | bytes 589824 | tf_op jit(solution)/shard_map/all_to_all | solution.py:33
  64.2 0.1 broadcast_and_fusion
  64.3 11.4 %all-to-all-done.1 = bf16[16,3,24,128]{3,2,1,0:T(8,128)(2,1)S(1)} async-done(((bf16[16,3,24,128]{3,2,1,0:T(8,128)(2,1)}), bf16[16,3,24,128]{3,2,1,0:T(8,128)(2,1)S(1)}, u32[]{:S(2)}, u32[]{:S(2)}) %all-to-all-start.1) | async-done | bytes 294944 | tf_op jit(solution)/shard_map/all_to_all | solution.py:33
  75.7 0.1 maximum_bitcast_fusion
  75.8 0.0 copy-done.2
  75.8 0.0 copy-done.3
  75.8 0.0 copy-done.4
  75.8 0.0 copy-done.5
  75.9 2.9 %fusion.42 = (bf16[2304,512]{1,0:T(8,128)(2,1)S(1)}, f32[2304,512]{1,0:T(8,128)}) fusion(bf16[2304,128]{1,0:T(8,128)(2,1)S(1)} %bitcast.53, bf16[128,128]{1,0:T(8,128)(2,1)S(1)} %copy-done.2, bf16[128,128]{1,0:T(8,128)(2,1)S(1)} %copy-done.3, bf16[128,128]{1,0:T(8,128)(2,1)S(1)} %copy-done.4, bf16[128,128]{1,0:T(8,128)(2,1)S(1)} %copy-done.5), kind=kOutput, calls=%fused_computation.53 | convolution fusion | flops 303693824 | bytes 7798784 | tf_op jit(solution)/shard_map/dot_general | solution.py:74
  78.8 0.1 fusion.40
  78.9 0.2 copy.73
  79.1 1.0 reshape_reshape.15
  80.1 1.4 fusion.18
  81.5 0.2 copy.72
  81.8 1.1 reshape_reshape.14
  82.9 0.2 copy.71
  83.1 1.0 reshape_reshape.13
  84.1 1.6 all-gather.2.cloned.1.call-done
  85.7 6.7 %copy_convert_fusion = f32[4,768,768]{2,1,0:T(8,128)} fusion(bf16[4,768,768]{2,0,1:T(4,128)(2,1)} %all-gather.2.cloned.1.call-done), kind=kLoop, calls=%fused_computation.7 | loop fusion | flops 2359296 | bytes 14155776 | tf_op jit(solution)/shard_map/convert_element_type | solution.py:95
  92.5 9.7 %copy.80 = f32[4,768,768]{1,2,0:T(8,128)} copy(f32[4,768,768]{2,1,0:T(8,128)} %copy_convert_fusion) | data formatting | bytes 18874368 | tf_op jit(solution)/shard_map/convert_element_type | solution.py:95
  102.1 0.0 copy-start.1
  102.1 15.4 %fusion = (f32[3,4,768]{2,1,0:T(4,128)S(1)}, f32[3,4,768,768]{2,3,1,0:T(8,128)}) fusion(f32[4,768,768]{1,2,0:T(8,128)} %copy.80, pred[768]{0:T(1024)(128)(4,1)S(1)} %iota_compare_fusion, bf16[3,768,4,32]{1,0,3,2:T(4,128)(2,1)} %reshape_reshape.15, bf16[3,768,4,32]{1,0,3,2:T(4,128)(2,1)} %reshape_reshape.14), kind=kOutput, calls=%fused_computation.2 | convolution fusion | flops 474209280 | bytes 38966016 | tf_op jit(solution)/shard_map/ijhd,ikhd->ihjk/dot_general | solution.py:92
  117.5 0.0 copy-done.1
  117.5 12.8 %fusion.1 = f32[3,4,768]{2,1,0:T(4,128)S(1)} fusion(f32[3,4,768,768]{2,3,1,0:T(8,128)} %get-tuple-element.12, f32[3,4,768]{2,1,0:T(4,128)S(1)} %get-tuple-element.11, f32[4,768,768]{1,2,0:T(8,128)S(1)} %copy-done.1, pred[768]{0:T(1024)(128)(4,1)S(1)} %iota_compare_fusion), kind=kLoop, calls=%fused_computation.3 | loop fusion | flops 28302336 | bytes 37823232 | tf_op jit(solution)/shard_map/reduce_sum | solution.py:99
  130.3 15.3 %fusion.12 = f32[3,768,4,32]{1,3,2,0:T(8,128)S(1)} fusion(f32[3,4,768,768]{2,3,1,0:T(8,128)} %get-tuple-element.12, f32[3,4,768]{2,1,0:T(4,128)S(1)} %get-tuple-element.11, f32[4,768,768]{1,2,0:T(8,128)} %copy.80, pred[768]{0:T(1024)(128)(4,1)S(1)} %iota_compare_fusion, bf16[3,768,4,32]{1,0,3,2:T(4,128)(2,1)} %reshape_reshape.13, f32[3,768,4]{1,2,0:T(4,128)S(1)} %bitcast.55), kind=kOutput, calls=%fused_computation.15 | convolution fusion | flops 481591296 | bytes 39592704 | tf_op jit(solution)/shard_map/ihjk,ikhd->ijhd/dot_general | solution.py:101
  145.7 0.8 copy.83
  146.5 0.2 copy.90
  146.7 0.4 copy.84
  147.1 1.6 multiply_convert_fusion
  148.7 0.0 copy-done
  148.7 0.5 fusion.11
  149.2 0.5 copy.85
  149.7 32.8 %all_to_all.35 = bf16[3,768,128]{2,0,1:T(4,128)(2,1)S(1)} all-to-all(bf16[3,768,128]{2,0,1:T(4,128)(2,1)S(1)} %copy.85), channel_id=1, replica_groups=mesh['row'=16,'col'=16] {'col'}, dimensions={1} | all-to-all | bytes 1179648 | tf_op jit(solution)/shard_map/all_to_all | solution.py:113
  182.5 0.9 copy.86
  (5 shorter events, 0.1 us)
Async XLA Ops:
  6.5 142.1 %copy-start = (bf16[128,128]{1,0:T(8,128)(2,1)S(1)}, bf16[128,128]{1,0:T(8,128)(2,1)}, u32[]{:S(2)}) copy-start(bf16[128,128]{1,0:T(8,128)(2,1)} %param.16) | copy-start | bytes 98308
  6.5 79.2 %all-gather.2.cloned.1.call-start = ((), (), s32[]{:S(2)}) async-start(), calls=%async_computation.4 | async-start | bytes 5013504 | tf_op jit(solution)/shard_map/all_gather | solution.py:90
  40.1 35.7 %copy-start.2 = (bf16[128,128]{1,0:T(8,128)(2,1)S(1)}, bf16[128,128]{1,0:T(8,128)(2,1)}, u32[]{:S(2)}) copy-start(bf16[128,128]{1,0:T(8,128)(2,1)} %param.14) | copy-start | bytes 98308
  40.1 35.7 %copy-start.3 = (bf16[128,128]{1,0:T(8,128)(2,1)S(1)}, bf16[128,128]{1,0:T(8,128)(2,1)}, u32[]{:S(2)}) copy-start(bf16[128,128]{1,0:T(8,128)(2,1)} %param.13) | copy-start | bytes 98308
  40.1 35.7 %copy-start.4 = (bf16[128,128]{1,0:T(8,128)(2,1)S(1)}, bf16[128,128]{1,0:T(8,128)(2,1)}, u32[]{:S(2)}) copy-start(bf16[128,128]{1,0:T(8,128)(2,1)} %param.12) | copy-start | bytes 98308
  40.1 35.7 %copy-start.5 = (bf16[128,128]{1,0:T(8,128)(2,1)S(1)}, bf16[128,128]{1,0:T(8,128)(2,1)}, u32[]{:S(2)}) copy-start(bf16[128,128]{1,0:T(8,128)(2,1)} %param.11) | copy-start | bytes 98308
  59.8 15.9 %all-to-all-start.1 = ((bf16[16,3,24,128]{3,2,1,0:T(8,128)(2,1)}), bf16[16,3,24,128]{3,2,1,0:T(8,128)(2,1)S(1)}, u32[]{:S(2)}, u32[]{:S(2)}) async-start(bf16[16,3,24,128]{3,2,1,0:T(8,128)(2,1)} %get-tuple-element.8), calls=%async_computation.1 | async-start | bytes 589824 | tf_op jit(solution)/shard_map/all_to_all | solution.py:33
  102.1 15.4 %copy-start.1 = (f32[4,768,768]{1,2,0:T(8,128)S(1)}, f32[4,768,768]{1,2,0:T(8,128)}, u32[]{:S(2)}) copy-start(f32[4,768,768]{1,2,0:T(8,128)} %copy.80) | copy-start | bytes 28311556
Sparse Core Ops, SparseCore 0:
  43.2 42.4 all-gather.1
where the time goes:
time: 191 us; the launch traced here: 190 us
  blocking collectives  73.7 us (39%)
  matrix products  35.5 us (19%)
  other arithmetic  27.7 us (15%)
  local copies, waits for them, and re-layouts  22.4 us (12%)
  between operations  14.3 us (7%)
  waiting for transfers between devices  13 us (7%)
  starting transfers between devices  3.72 us (2%)
    all_to_all x1, blocking collectives, per_device(): lax.all_to_all(update, 'col', split_axis=1, concat_axis=0, tiled=True)  32.8 us
    all_to_all x1, blocking collectives, from_everyone(): lax.all_to_all(jnp.broadcast_to(value[None], (length, *value.shape)), axi...  25 us
    all_to_all x1, blocking collectives, several_exchanges(): lax.all_to_all(slab, axis, split_axis=0, concat_axis=0, tiled=True)  15.9 us
    dot_general x1, matrix products, per_device(): jnp.einsum('ijhd,ikhd->ihjk', query_heads, key_heads, preferred_element_t...  15.4 us
    dot_general x1, matrix products, per_device(): jnp.einsum('ihjk,ikhd->ijhd', weights, value_heads, preferred_element_typ...  15.3 us
    reduce_sum x1, other arithmetic, per_device(): totals = jnp.sum(exponent, -1)  12.8 us
    all_to_all x1, waiting for transfers between devices, several_exchanges(): lax.all_to_all(slab, axis, split_axis=0, concat_axis=0, tiled=True)  11.4 us
    convert_element_type x1, local copies, waits for them, and re-layouts, per_device(): scores = scores + portion.astype(jnp.float32)[None]  9.65 us
  transfers between devices with their start and end apart: 2, of which 2 were waited for; matrix products, arithmetic and copies ran while one was open for 5% of the time, Pallas kernels for 0%

commit v1 on v0

v1 whole, which is shorter than its diff:
```python
import functools
import jax
import jax.numpy as jnp
from jax import lax
from jax.experimental import pallas as pl
from jax.experimental.pallas import tpu as pltpu
from jax.sharding import Mesh, PartitionSpec as P

epsilon = 1e-05
bf16, f32 = jnp.bfloat16, jnp.float32


def contract(a, b, da, db):
    return lax.dot_general(a, b, (((da,), (db,)), ((), ())), preferred_element_type=f32)


def prepare(pair_ref, gain_ref, wide_ref, normed_ref, bias_ref, *, step):
    rows, cols, channels = pair_ref.shape
    half = cols // 2
    lanes = wide_ref.shape[1]
    gain = gain_ref[...]
    lane = lax.broadcasted_iota(jnp.int32, (half, lanes), 1)
    first = lane < lanes // 2
    lane_j = lax.rem(lane, rows)

    def chunk(g, acc):
        start = g * step
        x = pair_ref[pl.ds(start, step)].reshape(step * cols, channels).astype(f32)
        centred = x - jnp.mean(x, -1, keepdims=True)
        spread = jnp.mean(centred * centred, -1, keepdims=True)
        normed = (centred * lax.rsqrt(spread + epsilon) * gain).astype(bf16)
        normed_ref[pl.ds(start, step)] = normed.reshape(step, cols, channels)
        wide = contract(normed, wide_ref[...], 1, 0)
        for t in range(step):
            one = wide[t * cols : (t + 1) * cols]
            both = jnp.where(first, one[:half], one[half:])
            acc = jnp.where(lane_j == start + t, both, acc)
        return acc

    bias = lax.fori_loop(0, rows // step, chunk, jnp.zeros((half, lanes), f32)).astype(bf16)
    for c in range(bias_ref.shape[0]):
        bias_ref[c] = bias


def attend(scalars, own_ref, other_ref, bias_ref, wq_ref, wk_ref, wv_ref, wg_ref, wo_ref, out_ref,
           table, rows_buf, key_buf, value_buf, gated_buf, *, heads, scale):
    length, core = scalars[0], scalars[1]
    blocks, each, width, channels = own_ref.shape
    slots = bias_ref.shape[0]
    half = width // 2
    head = channels // heads
    keys, queries = blocks * width, slots * width

    def build(c, carry):
        pieces = [bias_ref[q, c].astype(f32) for q in range(slots)]
        for kh in range(2):
            start = pl.multiple_of(c * width + kh * half, 8)
            pos = start + lax.broadcasted_iota(jnp.int32, (half, queries), 0)
            for h in range(heads):
                lo = (kh * heads + h) * width
                joined = jnp.concatenate([p[:, lo : lo + width] for p in pieces], axis=1)
                table[h, pl.ds(start, half), :] = jnp.where(pos < length, joined, -1e30)
        return carry

    lax.fori_loop(0, blocks, build, 0)
    lane = lax.broadcasted_iota(jnp.int32, (queries, channels), 1)

    def one_row(n, carry):
        side, t = n // each, lax.rem(n, each)

        @pl.when(side == 0)
        def _():
            for c in range(blocks):
                rows_buf[c * width : (c + 1) * width] = own_ref[c, t]

        @pl.when(side == 1)
        def _():
            for c in range(blocks):
                rows_buf[c * width : (c + 1) * width] = other_ref[c, t]

        rows = rows_buf[...]
        key_buf[...] = contract(rows, wk_ref[...], 1, 0).astype(bf16)
        value_buf[...] = contract(wv_ref[...], rows, 1, 1).astype(bf16)
        asked = jnp.concatenate(
            [rows_buf[pl.ds(pl.multiple_of((2 * q + core) * width, 16), width)] for q in range(slots)], axis=0
        )
        query = (contract(asked, wq_ref[...], 1, 0) * scale).astype(bf16)
        gating = jax.nn.sigmoid(contract(wg_ref[...], asked, 1, 1)).astype(bf16).astype(f32)
        for h in range(heads):
            mine = jnp.where((lane >= h * head) & (lane < (h + 1) * head), query, jnp.zeros_like(query))
            scores = contract(key_buf[...], mine, 1, 1) + table[h]
            highest = jnp.max(scores, 0, keepdims=True)
            exponent = jnp.exp(scores - highest)
            totals = jnp.sum(exponent, 0, keepdims=True)
            blended = contract(value_buf[h * head : (h + 1) * head], exponent.astype(bf16), 1, 0)
            blended = blended / totals
            gated_buf[h * head : (h + 1) * head] = (gating[h * head : (h + 1) * head] * blended).astype(bf16)
        update = contract(gated_buf[...], wo_ref[...], 0, 0)
        row_base = jnp.where(side == 0, scalars[2], scalars[3])
        row_ok = row_base + t < length
        place = lax.broadcasted_iota(jnp.int32, (width, channels), 0)
        for q in range(slots):
            ok = (place + (2 * q + core) * width < length) & row_ok
            piece = update[q * width : (q + 1) * width]
            out_ref[side, q, t] = jnp.where(ok, piece, 0.0).astype(bf16)
        return carry

    lax.fori_loop(0, 2 * each, one_row, 0)


ROW, COL, SLOT = ("z_lo", "x", "core"), ("y", "z_hi"), ("z_lo", "x")
VMEM = pl.BlockSpec(memory_space=pltpu.VMEM)
SMEM = pl.BlockSpec(memory_space=pltpu.SMEM)


def run_prepare(pair, ln_gain, w_bias, across):
    tile_rows, tile_cols, channels = pair.shape
    heads = w_bias.shape[1]
    half = tile_cols // 2
    lanes = 2 * heads * tile_rows
    wide = jnp.tile(jnp.repeat(w_bias, tile_rows, axis=1), (1, 2))
    return pl.pallas_call(
        functools.partial(prepare, step=4),
        out_shape=(
            jax.ShapeDtypeStruct(pair.shape, bf16),
            jax.ShapeDtypeStruct((across, half, lanes), bf16),
        ),
        in_specs=[VMEM] * 3,
        out_specs=(VMEM, VMEM),
        name="prepare",
    )(pair, ln_gain.reshape(1, channels), wide)


def run_attend(scalars, own, other, bias, wq, wk, wv, wg, wo, heads):
    blocks, each, width, channels = own.shape
    slots = bias.shape[0]
    keys, queries = blocks * width, slots * width
    head = channels // heads
    return pl.pallas_call(
        functools.partial(attend, heads=heads, scale=head**-0.5),
        out_shape=jax.ShapeDtypeStruct((2, slots, each, width, channels), bf16),
        in_specs=[SMEM] + [VMEM] * 8,
        out_specs=VMEM,
        scratch_shapes=[
            pltpu.VMEM((heads, keys, queries), f32),
            pltpu.VMEM((keys, channels), bf16),
            pltpu.VMEM((keys, channels), bf16),
            pltpu.VMEM((channels, keys), bf16),
            pltpu.VMEM((channels, queries), bf16),
        ],
        compiler_params=pltpu.CompilerParams(vmem_limit_bytes=48 << 20),
        cost_estimate=pl.CostEstimate(flops=2_500_000_000, transcendentals=7_000_000, bytes_accessed=4_000_000),
        name="attend",
    )(scalars, own, other, bias, wq, wk, wv, wg, wo)


def everyone(value, axes, count):
    spread = jnp.broadcast_to(value[None], (count, *value.shape))
    return lax.all_to_all(spread, axes, 0, 0, tiled=True)


def per_device(pair, ln_gain, w_query, w_key, w_value, w_gate, w_bias, w_out, valid_length):
    tile_rows, tile_cols, channels = pair.shape
    heads = w_bias.shape[1]
    across = lax.axis_size(COL)
    slots = lax.axis_size(SLOT)
    each = tile_rows // across
    swap = [(0, 1), (1, 0)]
    normed, bias = run_prepare(pair, ln_gain, w_bias, across)
    bias = lax.all_to_all(bias, COL, 0, 0, tiled=True)
    bias = everyone(bias, SLOT, slots)
    own = lax.all_to_all(normed.reshape(across, each, tile_cols, channels), COL, 0, 0, tiled=True)
    other = lax.ppermute(own, "core", swap)
    core = lax.axis_index("core")
    slot = lax.axis_index(SLOT)
    base = lax.axis_index(COL) * each
    own_base = (2 * slot + core) * tile_rows + base
    other_base = (2 * slot + 1 - core) * tile_rows + base
    scalars = jnp.stack([valid_length[0], core, own_base, other_base]).astype(jnp.int32)
    out = run_attend(scalars, own, other, bias, w_query, w_key, w_value.T, w_gate.T, w_out, heads)
    theirs = lax.ppermute(out[1], "core", swap)
    mine = out[0]
    even = jnp.where(core == 0, mine, theirs)
    odd = jnp.where(core == 0, theirs, mine)
    update = jnp.stack([even, odd], axis=1).reshape(across, each, tile_cols, channels)
    update = lax.all_to_all(update, COL, 0, 0, tiled=True)
    return update.reshape(tile_rows, tile_cols, channels)


def solution(mesh):
    fine = Mesh(mesh.devices.reshape(2, 4, 2, 4, 4), ROW + COL)
    placed = (P(ROW, COL, None), P(), P(), P(), P(), P(), P(), P(), P())
    return jax.shard_map(
        per_device, mesh=fine, in_specs=placed, out_specs=P(ROW, COL, None), check_vma=False
    )
```

time: 191 us -> 142 us (0.74)
  matrix products: 35.5 us -> 0 us
  other arithmetic: 27.7 us -> 0.18 us
  Pallas kernels: 0 us -> 25.8 us
  between operations: 14.3 us -> 0.72 us
  waiting for transfers between devices: 13 us -> 23 us
  local copies, waits for them, and re-layouts: 22.4 us -> 12.7 us
    dot_general x5 -> x0, matrix products: 35.5 us -> none  [the longest x1 15.4 us: per_device(): jnp.einsum('ijhd,ikhd->ihjk', query_heads, key_heads, preferred_element_t...]
    pallas_call x0 -> x2, Pallas kernels: none -> 25.8 us  [the longest x1 19.5 us: run_attend(): pl.pallas_call(functools.partial(attend, heads=heads, scale=head ** (-0.5...]
    reduce_sum x3 -> x0, other arithmetic: 16 us -> none  [the longest x1 12.8 us: per_device(): totals = jnp.sum(exponent, -1)]
    convert_element_type x4 -> x0, other arithmetic: 11.5 us -> none  [the longest x1 6.74 us: per_device(): scores = scores + portion.astype(jnp.float32)[None]]
    convert_element_type x4 -> x0, local copies, waits for them, and re-layouts: 10.5 us -> none  [the longest x1 9.65 us: per_device(): scores = scores + portion.astype(jnp.float32)[None]]
    all_to_all x1, waiting for transfers between devices: 11.4 us -> 21.4 us  [everyone(): return lax.all_to_all(spread, axes, 0, 0, tiled=True)]
    unnamed x16 -> x17, local copies, waits for them, and re-layouts: 2.34 us -> 9.42 us
    reshape x3 -> x0, local copies, waits for them, and re-layouts: 3.25 us -> none  [the longest x2 2.89 us: in_order(): return jnp.moveaxis(blocks, 0, dim).reshape(lengths)]
  transfers between devices with their start and end apart: 2 -> 3, of which waited for: 2 -> 2; matrix products, arithmetic and copies ran while one was open for 5% -> 2% of each run, Pallas kernels for 0% -> 0%
where the time goes in v1:
time: 142 us; the launch traced here: 141 us
  blocking collectives  73.1 us (51%)
  Pallas kernels  25.8 us (18%)
  waiting for transfers between devices  23 us (16%)
  local copies, waits for them, and re-layouts  12.7 us (9%)
  starting transfers between devices  5.19 us (4%)
    all_to_all x1, blocking collectives, per_device(): bias = lax.all_to_all(bias, COL, 0, 0, tiled=True)  25.2 us
    all_to_all x1, blocking collectives, per_device(): update = lax.all_to_all(update, COL, 0, 0, tiled=True)  24.9 us
    all_to_all x1, blocking collectives, per_device(): lax.all_to_all(normed.reshape(across, each, tile_cols, channels), COL, 0,...  23.1 us
    all_to_all x1, waiting for transfers between devices, everyone(): return lax.all_to_all(spread, axes, 0, 0, tiled=True)  21.4 us
    pallas_call x1, Pallas kernels, run_attend(): pl.pallas_call(functools.partial(attend, heads=heads, scale=head ** (-0.5...  19.5 us
    unnamed x17, local copies, waits for them, and re-layouts  9.42 us
    pallas_call x1, Pallas kernels, run_prepare(): pl.pallas_call(functools.partial(prepare, step=4), out_shape=(jax.ShapeDt...  6.33 us
    all_to_all x1, starting transfers between devices, everyone(): return lax.all_to_all(spread, axes, 0, 0, tiled=True)  5.1 us
  transfers between devices with their start and end apart: 3, of which 2 were waited for; matrix products, arithmetic and copies ran while one was open for 2% of the time, Pallas kernels for 0%

profile of v1, /device:TPU:2, one launch (start us, length us, event | category | flops | bytes accessed | tf_op | source)
XLA Modules:
  0.0 140.6 jit_solution(1766635133008231716)
XLA Ops:
  0.0 0.7 broadcast_in_dim.4
  0.7 0.8 copy.13.wide_ref
  1.5 6.3 %prepare.1 = (bf16[48,48,128]{2,1,0:T(8,128)(2,1)}, bf16[16,24,384]{2,1,0:T(8,128)(2,1)}) custom-call(bf16[48,48,128]{2,1,0:T(8,128)(2,1)} %pair_ref.1, f32[1,128]{1,0:T(1,128)} %bitcast.30, bf16[128,384]{1,0:T(8,128)(2,1)} %copy.13.wide_ref), custom_call_target="tpu_custom_call" | custom-call | tf_op jit(solution)/shard_map/prepare/pallas_call | solution.py:122
  7.8 25.2 %all_to_all.20 = bf16[16,24,384]{2,1,0:T(8,128)(2,1)S(1)} all-to-all(bf16[16,24,384]{2,1,0:T(8,128)(2,1)} %get-tuple-element.8), channel_id=1, replica_groups=mesh['z_lo'=2,'x'=4,'core'=2,'y'=4,'z_hi'=4] {'y','z_hi'}, dimensions={0} | all-to-all | bytes 589824 | tf_op jit(solution)/shard_map/all_to_all | solution.py:170
  32.9 23.1 %all_to_all.21.own_ref = bf16[16,3,48,128]{3,2,1,0:T(8,128)(2,1)S(1)} all-to-all(bf16[16,3,48,128]{3,2,1,0:T(8,128)(2,1)} %bitcast.27), channel_id=1, replica_groups=mesh['z_lo'=2,'x'=4,'core'=2,'y'=4,'z_hi'=4] {'y','z_hi'}, dimensions={0} | all-to-all | bytes 1179648 | tf_op jit(solution)/shard_map/all_to_all | solution.py:172
  56.1 1.7 %broadcast_in_dim.10 = bf16[8,16,24,384]{3,2,1,0:T(8,128)(2,1)} broadcast(bf16[16,24,384]{2,1,0:T(8,128)(2,1)S(1)} %all_to_all.20), dimensions={1,2,3} | broadcast | bytes 2654208 | tf_op jit(solution)/shard_map/broadcast_in_dim | solution.py:158
  57.8 5.1 %all-to-all-start.2 = ((bf16[8,16,24,384]{3,2,1,0:T(8,128)(2,1)}), bf16[8,16,24,384]{3,2,1,0:T(8,128)(2,1)S(1)}, u32[]{:S(2)}, u32[]{:S(2)}) async-start(bf16[8,16,24,384]{3,2,1,0:T(8,128)(2,1)} %broadcast_in_dim.10), calls=%async_computation.2 | async-start | bytes 4718592 | tf_op jit(solution)/shard_map/all_to_all | solution.py:159
  62.9 0.0 collective-permute-start
  63.5 1.5 %copy.14 = bf16[128,128]{0,1:T(8,128)(2,1)} copy(bf16[128,128]{1,0:T(8,128)(2,1)} %param.13) | data formatting | bytes 65536 | tf_op args[4]
  65.0 1.5 %copy.15 = bf16[128,128]{0,1:T(8,128)(2,1)} copy(bf16[128,128]{1,0:T(8,128)(2,1)} %param.14) | data formatting | bytes 65536 | tf_op args[5]
  66.5 0.1 pad_add_fusion.scalars
  66.5 0.0 collective-permute-done.other_ref
  66.5 0.0 copy-start.2
  66.5 0.8 copy-done.2
  67.4 21.4 %all-to-all-done.2.bias_ref = bf16[8,16,24,384]{3,2,1,0:T(8,128)(2,1)S(1)} async-done(((bf16[8,16,24,384]{3,2,1,0:T(8,128)(2,1)}), bf16[8,16,24,384]{3,2,1,0:T(8,128)(2,1)S(1)}, u32[]{:S(2)}, u32[]{:S(2)}) %all-to-all-start.2) | async-done | bytes 2359328 | tf_op jit(solution)/shard_map/all_to_all | solution.py:159
  88.7 0.0 copy-start
  88.8 0.8 copy-done
  89.5 0.0 copy-start.1
  89.5 0.8 copy-done.1
  90.3 0.0 copy-start.3
  90.3 1.1 copy-done.3
  91.3 0.0 copy-start.4
  91.3 0.8 copy-done.4
  92.1 0.0 copy-start.5
  92.1 0.8 copy-done.5
  92.8 0.0 copy-start.6
  92.8 0.8 copy-done.6
  93.6 19.5 %attend.1 = bf16[2,8,3,48,128]{4,3,2,1,0:T(8,128)(2,1)S(1)} custom-call(s32[4]{0:T(128)S(1)} %pad_add_fusion.scalars, bf16[16,3,48,128]{3,2,1,0:T(8,128)(2,1)S(1)} %all_to_all.21.own_ref, bf16[16,3,48,128]{3,2,1,0:T(8,128)(2,1)S(1)} %copy-done.3, bf16[8,16,24,384]{3,2,1,0:T(8,128)(2,1)S(1)} %all-to-all-done.2.bias_ref, bf16[128,128]{1,0:T(8,128)(2,1)S(1)} %copy-done.4, ...), custom_call_target="tpu_custom_call" | custom-call | flops 2500000000 | bytes 4000000 | tf_op jit(solution)/shard_map/attend/pallas_call | solution.py:139
  113.1 0.1 collective-permute-start.1
  113.2 1.6 %collective-permute-done.1 = bf16[8,3,48,128]{3,2,1,0:T(8,128)(2,1)S(1)} collective-permute-done((bf16[8,3,48,128]{3,2,1,0:T(8,128)(2,1)S(1)}, bf16[8,3,48,128]{3,2,1,0:T(8,128)(2,1)S(1)}, u32[]{:S(2)}, u32[]{:S(2)}) %collective-permute-start.1) | collective-permute-done | bytes 294944 | tf_op jit(solution)/shard_map/ppermute | solution.py:181
  114.8 0.1 pad_maximum_fusion
  114.9 24.9 %all_to_all.22 = bf16[16,3,48,128]{3,2,1,0:T(8,128)(2,1)S(1)} all-to-all(bf16[16,3,48,128]{3,2,1,0:T(8,128)(2,1)S(1)} %bitcast.25), channel_id=1, replica_groups=mesh['z_lo'=2,'x'=4,'core'=2,'y'=4,'z_hi'=4] {'y','z_hi'}, dimensions={0} | all-to-all | bytes 1179648 | tf_op jit(solution)/shard_map/all_to_all | solution.py:186
  139.8 0.8 copy.19
  (4 shorter events, 0.1 us)
Async XLA Ops:
  57.8 31.0 %all-to-all-start.2 = ((bf16[8,16,24,384]{3,2,1,0:T(8,128)(2,1)}), bf16[8,16,24,384]{3,2,1,0:T(8,128)(2,1)S(1)}, u32[]{:S(2)}, u32[]{:S(2)}) async-start(bf16[8,16,24,384]{3,2,1,0:T(8,128)(2,1)} %broadcast_in_dim.10), calls=%async_computation.2 | async-start | bytes 4718592 | tf_op jit(solution)/shard_map/all_to_all | solution.py:159
  62.9 3.7 %collective-permute-start = (bf16[16,3,48,128]{3,2,1,0:T(8,128)(2,1)S(1)}, bf16[16,3,48,128]{3,2,1,0:T(8,128)(2,1)S(1)}, u32[]{:S(2)}, u32[]{:S(2)}) collective-permute-start(bf16[16,3,48,128]{3,2,1,0:T(8,128)(2,1)S(1)} %all_to_all.21.own_ref), channel_id=1, source_target_pairs={{0,16},{16,0},{1,17},{17,1},{2,18},{18,2},{3,19},{19,3},{4,20},{20... | collective-permute-start | bytes 1769480 | tf_op jit(solution)/shard_map/ppermute | solution.py:173
  66.5 0.8 copy-start.2
  88.7 0.8 copy-start
  89.5 0.8 copy-start.1
  90.3 1.1 copy-start.3
  91.3 0.8 copy-start.4
  92.1 0.8 copy-start.5
  92.8 0.8 copy-start.6
  113.1 1.7 %collective-permute-start.1 = (bf16[8,3,48,128]{3,2,1,0:T(8,128)(2,1)S(1)}, bf16[8,3,48,128]{3,2,1,0:T(8,128)(2,1)S(1)}, u32[]{:S(2)}, u32[]{:S(2)}) collective-permute-start(bf16[8,3,48,128]{3,2,1,0:T(8,128)(2,1)S(1)} %slice_bitcast_fusion), channel_id=1, source_target_pairs={{0,16},{16,0},{1,17},{17,1},{2,18},{18,2},{3,19},{19,3},{4,20},{20... | collective-permute-start | bytes 884744 | tf_op jit(solution)/shard_map/ppermute | solution.py:181

commit v2 on v1

v2 whole, which is shorter than its diff:
```python
import functools
import jax
import jax.numpy as jnp
from jax import lax
from jax.experimental import pallas as pl
from jax.experimental.pallas import tpu as pltpu
from jax.sharding import Mesh, PartitionSpec as P

epsilon = 1e-05
bf16, f32 = jnp.bfloat16, jnp.float32


def contract(a, b, da, db):
    return lax.dot_general(a, b, (((da,), (db,)), ((), ())), preferred_element_type=f32)


def prepare(pair_ref, gain_ref, w_ref, normed_ref, bias_ref, wide_ref, *, step):
    rows, cols, channels = pair_ref.shape
    heads = w_ref.shape[1]
    half = cols // 2
    lanes = wide_ref.shape[1]
    gain = gain_ref[...]
    of_head = lax.rem(lax.broadcasted_iota(jnp.int32, (channels, lanes), 1) // rows, heads)
    weight = w_ref[...].astype(f32)
    wide = jnp.zeros((channels, lanes), f32)
    for h in range(heads):
        wide = jnp.where(of_head == h, weight[:, h : h + 1], wide)
    wide_ref[...] = wide.astype(bf16)
    lane = lax.broadcasted_iota(jnp.int32, (half, lanes), 1)
    first = lane < lanes // 2
    lane_j = lax.rem(lane, rows)

    def chunk(g, acc):
        start = g * step
        x = pair_ref[pl.ds(start, step)].reshape(step * cols, channels).astype(f32)
        centred = x - jnp.mean(x, -1, keepdims=True)
        spread = jnp.mean(centred * centred, -1, keepdims=True)
        normed = (centred * lax.rsqrt(spread + epsilon) * gain).astype(bf16)
        normed_ref[pl.ds(start, step)] = normed.reshape(step, cols, channels)
        wide = contract(normed, wide_ref[...], 1, 0)
        for t in range(step):
            one = wide[t * cols : (t + 1) * cols]
            both = jnp.where(first, one[:half], one[half:])
            acc = jnp.where(lane_j == start + t, both, acc)
        return acc

    bias = lax.fori_loop(0, rows // step, chunk, jnp.zeros((half, lanes), f32)).astype(bf16)
    for c in range(bias_ref.shape[0]):
        bias_ref[c] = bias


def gate(*refs):
    refs[-1][...] = jnp.zeros_like(refs[-1])


def attend(length_ref, own_ref, other_ref, *refs, heads, scale, slots):
    parts_hbm, weights_hbm, refs = refs[:slots], refs[slots : slots + 5], refs[slots + 6 :]
    out_ref, weights, sems, parts, part_sems, table, rows_buf, key_buf, value_buf, gated_buf = refs
    fetches = [pltpu.make_async_copy(p, parts.at[n], part_sems.at[n]) for n, p in enumerate(parts_hbm)]
    copies = [pltpu.make_async_copy(w, weights.at[n], sems.at[n]) for n, w in enumerate(weights_hbm)]
    for copy in fetches + copies:
        copy.start()
    length = length_ref[0]
    blocks, each, width, channels = own_ref.shape
    head = channels // heads
    queries = slots * width
    core, x, z = lax.axis_index("core"), lax.axis_index("x"), lax.axis_index("z_lo")
    along = lax.axis_size("x")
    places = [zz * along + lax.rem(x + by, along) for zz, by in order_of_slots(z, along)]
    block_of = [2 * p + core for p in places]
    base = (lax.axis_index("y") * lax.axis_size("z_hi") + lax.axis_index("z_hi")) * each
    own_base = (2 * (z * along + x) + core) * (each * blocks) + base
    other_base = (2 * (z * along + x) + 1 - core) * (each * blocks) + base
    half = width // 2
    for copy in fetches:
        copy.wait()

    def build(c, carry):
        pieces = [parts[n, c].astype(f32) for n in range(slots)]
        for kh in range(2):
            start = pl.multiple_of(c * width + kh * half, 8)
            pos = start + lax.broadcasted_iota(jnp.int32, (half, queries), 0)
            for h in range(heads):
                lo = (kh * heads + h) * width
                joined = jnp.concatenate([p[:, lo : lo + width] for p in pieces], axis=1)
                table[h, pl.ds(start, half), :] = jnp.where(pos < length, joined, -1e30)
        return carry

    lax.fori_loop(0, blocks, build, 0)
    for copy in copies:
        copy.wait()
    wq, wk, wo = weights[0], weights[1], weights[4]
    wv = weights[2].T
    wg = weights[3].T
    lane = lax.broadcasted_iota(jnp.int32, (queries, channels), 1)

    def one_row(n, carry):
        side, t = n // each, lax.rem(n, each)

        @pl.when(side == 0)
        def _():
            for c in range(blocks):
                rows_buf[c * width : (c + 1) * width] = own_ref[c, t]

        @pl.when(side == 1)
        def _():
            for c in range(blocks):
                rows_buf[c * width : (c + 1) * width] = other_ref[c, t]

        rows = rows_buf[...]
        key_buf[...] = contract(rows, wk, 1, 0).astype(bf16)
        value_buf[...] = contract(wv, rows, 1, 1).astype(bf16)
        asked = jnp.concatenate(
            [rows_buf[pl.ds(pl.multiple_of(b * width, 16), width)] for b in block_of], axis=0
        )
        query = (contract(asked, wq, 1, 0) * scale).astype(bf16)
        gating = jax.nn.sigmoid(contract(wg, asked, 1, 1)).astype(bf16).astype(f32)
        for h in range(heads):
            mine = jnp.where((lane >= h * head) & (lane < (h + 1) * head), query, jnp.zeros_like(query))
            scores = contract(key_buf[...], mine, 1, 1) + table[h]
            highest = jnp.max(scores, 0, keepdims=True)
            exponent = jnp.exp(scores - highest)
            totals = jnp.sum(exponent, 0, keepdims=True)
            blended = contract(value_buf[h * head : (h + 1) * head], exponent.astype(bf16), 1, 0)
            blended = blended / totals
            gated_buf[h * head : (h + 1) * head] = (gating[h * head : (h + 1) * head] * blended).astype(bf16)
        update = contract(gated_buf[...], wo, 0, 0)
        row_base = jnp.where(side == 0, own_base, other_base)
        row_ok = row_base + t < length
        place = lax.broadcasted_iota(jnp.int32, (width, channels), 0)
        for s in range(slots):
            ok = (place + block_of[s] * width < length) & row_ok
            piece = update[s * width : (s + 1) * width]
            out_ref[side, places[s], t] = jnp.where(ok, piece, 0.0).astype(bf16)
        return carry

    lax.fori_loop(0, 2 * each, one_row, 0)


ROW, COL = ("z_lo", "x", "core"), ("y", "z_hi")
VMEM = pl.BlockSpec(memory_space=pltpu.VMEM)
HBM = pl.BlockSpec(memory_space=pltpu.HBM)
SMEM = pl.BlockSpec(memory_space=pltpu.SMEM)


def run_prepare(pair, ln_gain, w_bias, across):
    tile_rows, tile_cols, channels = pair.shape
    heads = w_bias.shape[1]
    half = tile_cols // 2
    lanes = 2 * heads * tile_rows
    return pl.pallas_call(
        functools.partial(prepare, step=16),
        out_shape=(
            jax.ShapeDtypeStruct(pair.shape, bf16),
            jax.ShapeDtypeStruct((across, half, lanes), bf16),
        ),
        in_specs=[VMEM] * 3,
        out_specs=(VMEM, VMEM),
        scratch_shapes=[pltpu.VMEM((channels, lanes), bf16)],
        compiler_params=pltpu.CompilerParams(vmem_limit_bytes=12 << 20),
        name="prepare",
    )(pair, ln_gain.reshape(1, channels), w_bias)


def order_of_slots(z, along):
    near = [(z, 0), (z, along - 1), (z, 1), (1 - z, 0)]
    return near + [(z, along - 2), (1 - z, along - 1), (1 - z, 1), (1 - z, 2)]


def run_gate(arrays):
    return pl.pallas_call(
        gate,
        out_shape=jax.ShapeDtypeStruct((8, 128), f32),
        in_specs=[HBM] * len(arrays),
        out_specs=VMEM,
        compiler_params=pltpu.CompilerParams(vmem_limit_bytes=1 << 20),
        name="gate",
    )(*arrays)


def run_attend(length, own, other, parts, weights, passed, heads):
    blocks, each, width, channels = own.shape
    slots = len(parts)
    keys, queries = blocks * width, slots * width
    head = channels // heads
    return pl.pallas_call(
        functools.partial(attend, heads=heads, scale=head**-0.5, slots=slots),
        out_shape=jax.ShapeDtypeStruct((2, slots, each, width, channels), bf16),
        in_specs=[SMEM] + [VMEM] * 2 + [HBM] * (slots + 6),
        out_specs=VMEM,
        scratch_shapes=[
            pltpu.VMEM((5, channels, channels), bf16),
            pltpu.SemaphoreType.DMA((5,)),
            pltpu.VMEM((slots, *parts[0].shape), bf16),
            pltpu.SemaphoreType.DMA((slots,)),
            pltpu.VMEM((heads, keys, queries), f32),
            pltpu.VMEM((keys, channels), bf16),
            pltpu.VMEM((keys, channels), bf16),
            pltpu.VMEM((channels, keys), bf16),
            pltpu.VMEM((channels, queries), bf16),
        ],
        compiler_params=pltpu.CompilerParams(vmem_limit_bytes=32 << 20),
        cost_estimate=pl.CostEstimate(flops=2_500_000_000, transcendentals=7_000_000, bytes_accessed=4_000_000),
        name="attend",
    )(length, own, other, *parts, *weights, passed)


def shifted(value, axis, by):
    n = lax.axis_size(axis)
    return lax.ppermute(value, axis, [(k, (k + by) % n) for k in range(n)])


def per_device_inner(pair, ln_gain, w_query, w_key, w_value, w_gate, w_bias, w_out, valid_length):
    tile_rows, tile_cols, channels = pair.shape
    heads = w_bias.shape[1]
    across = lax.axis_size(COL)
    each = tile_rows // across
    normed, bias = run_prepare(pair, ln_gain, w_bias, across)
    mine = lax.all_to_all(bias, COL, 0, 0, tiled=True)
    own = lax.all_to_all(normed.reshape(across, each, tile_cols, channels), COL, 0, 0, tiled=True)
    below = shifted(mine, "z_lo", 1)
    left = shifted(mine, "x", 1)
    right = shifted(mine, "x", -1)
    below_left = shifted(below, "x", 1)
    below_right = shifted(below, "x", -1)
    far = shifted(left, "x", 1)
    below_far = shifted(below_right, "x", -1)
    passed = run_gate([right, below_left, far, below_far])
    other = shifted(own, "core", 1)
    parts = [mine, left, right, below, far, below_left, below_right, below_far]
    weights = (w_query, w_key, w_value, w_gate, w_out)
    out = run_attend(valid_length, own, other, parts, weights, passed, heads)
    theirs = shifted(out[1], "core", 1)
    core = lax.axis_index("core")
    even = jnp.where(core == 0, out[0], theirs)
    odd = jnp.where(core == 0, theirs, out[0])
    update = jnp.stack([even, odd], axis=1).reshape(across, each, tile_cols, channels)
    update = lax.all_to_all(update, COL, 0, 0, tiled=True)
    return update.reshape(tile_rows, tile_cols, channels)


def solution(mesh):
    fine = Mesh(mesh.devices.reshape(2, 4, 2, 4, 4), ROW + COL)
    placed = (P(ROW, COL, None), P(), P(), P(), P(), P(), P(), P(), P())
    return jax.shard_map(per_device_inner, mesh=fine, in_specs=placed, out_specs=P(ROW, COL, None), check_vma=False)
```

time: 142 us -> 127 us (0.89)
  blocking collectives: 73.1 us -> 54.5 us
  waiting for transfers between devices: 23 us -> 33.3 us
  local copies, waits for them, and re-layouts: 12.7 us -> 3.43 us
  starting transfers between devices: 5.19 us -> 11.1 us
  Pallas kernels: 25.8 us -> 22.4 us
    ppermute x2 -> x9, waiting for transfers between devices: 1.57 us -> 32.7 us  [shifted(): return lax.ppermute(value, axis, [(k, (k + by) % n) for k in range(n)])]
    all_to_all x1, waiting for transfers between devices: 21.4 us -> 0.62 us  [per_device_inner(): lax.all_to_all(normed.reshape(across, each, tile_cols, channels), COL, 0,...]
    all_to_all x3 -> x2, blocking collectives: 73.1 us -> 54.5 us  [the longest x1 29.6 us: per_device_inner(): update = lax.all_to_all(update, COL, 0, 0, tiled=True)]
    ppermute x2 -> x9, starting transfers between devices: 0.1 us -> 7.53 us  [shifted(): return lax.ppermute(value, axis, [(k, (k + by) % n) for k in range(n)])]
    unnamed x17 -> x16, local copies, waits for them, and re-layouts: 9.42 us -> 3.37 us
    pallas_call x1 -> x2, Pallas kernels: 6.33 us -> 2.53 us  [the longest x1 2.53 us: run_prepare(): pl.pallas_call(functools.partial(prepare, step=16), out_shape=(jax.ShapeD...]
    broadcast_in_dim x2 -> x0, local copies, waits for them, and re-layouts: 2.41 us -> none  [the longest x1 1.72 us: everyone(): spread = jnp.broadcast_to(value[None], (count, *value.shape))]
    all_to_all x1, starting transfers between devices: 5.1 us -> 3.58 us  [per_device_inner(): lax.all_to_all(normed.reshape(across, each, tile_cols, channels), COL, 0,...]
  transfers between devices with their start and end apart: 3 -> 10, of which waited for: 2 -> 7; matrix products, arithmetic and copies ran while one was open for 2% -> 0% of each run, Pallas kernels for 0% -> 0%
where the time goes in v2:
time: 127 us; the launch traced here: 126 us
  blocking collectives  54.5 us (43%)
  waiting for transfers between devices  33.3 us (26%)
  Pallas kernels  22.4 us (18%)
  starting transfers between devices  11.1 us (9%)
  local copies, waits for them, and re-layouts  3.43 us (3%)
    ppermute x9, waiting for transfers between devices, shifted(): return lax.ppermute(value, axis, [(k, (k + by) % n) for k in range(n)])  32.7 us
    all_to_all x1, blocking collectives, per_device_inner(): update = lax.all_to_all(update, COL, 0, 0, tiled=True)  29.6 us
    all_to_all x1, blocking collectives, per_device_inner(): mine = lax.all_to_all(bias, COL, 0, 0, tiled=True)  24.9 us
    pallas_call x1, Pallas kernels, run_attend(): pl.pallas_call(functools.partial(attend, heads=heads, scale=head ** (-0.5...  19.9 us
    ppermute x9, starting transfers between devices, shifted(): return lax.ppermute(value, axis, [(k, (k + by) % n) for k in range(n)])  7.53 us
    all_to_all x1, starting transfers between devices, per_device_inner(): lax.all_to_all(normed.reshape(across, each, tile_cols, channels), COL, 0,...  3.58 us
    unnamed x16, local copies, waits for them, and re-layouts  3.37 us
  transfers between devices with their start and end apart: 10, of which 7 were waited for; matrix products, arithmetic and copies ran while one was open for 0% of the time, Pallas kernels for 0%

profile of v2, /device:TPU:2, one launch (start us, length us, event | category | flops | bytes accessed | tf_op | source)
XLA Modules:
  0.0 125.7 jit_solution(7935780775448254487)
XLA Ops:
  0.0 0.8 copy.11.w_ref
  0.8 0.0 copy-start.1
  0.8 0.7 copy-done.1
  1.5 0.0 copy-start
  1.5 1.1 copy-done
  2.5 2.5 %prepare.1 = (bf16[48,48,128]{2,1,0:T(8,128)(2,1)}, bf16[16,24,384]{2,1,0:T(8,128)(2,1)S(1)}) custom-call(bf16[48,48,128]{2,1,0:T(8,128)(2,1)S(1)} %copy-done, f32[1,128]{1,0:T(1,128)S(1)} %bitcast.16, bf16[128,4]{1,0:T(8,128)(2,1)S(1)} %copy.11.w_ref), custom_call_target="tpu_custom_call" | custom-call | tf_op jit(solution)/shard_map/prepare/pallas_call | solution.py:151
  5.1 24.9 %all_to_all.15.refs_0_ = bf16[16,24,384]{2,1,0:T(8,128)(2,1)S(1)} all-to-all(bf16[16,24,384]{2,1,0:T(8,128)(2,1)S(1)} %get-tuple-element.8), channel_id=1, replica_groups=mesh['z_lo'=2,'x'=4,'core'=2,'y'=4,'z_hi'=4] {'y','z_hi'}, dimensions={0} | all-to-all | bytes 589824 | tf_op jit(solution)/shard_map/all_to_all | solution.py:219
  30.0 3.6 %all-to-all-start = ((bf16[16,3,48,128]{3,2,1,0:T(8,128)(2,1)}), bf16[16,3,48,128]{3,2,1,0:T(8,128)(2,1)S(1)}, u32[]{:S(2)}, u32[]{:S(2)}) async-start(bf16[16,3,48,128]{3,2,1,0:T(8,128)(2,1)} %bitcast.1), calls=%async_computation | async-start | bytes 1179648 | tf_op jit(solution)/shard_map/all_to_all | solution.py:220
  33.6 1.1 collective-permute-start.3
  34.7 1.5 %collective-permute-start.1 = (bf16[16,24,384]{2,1,0:T(8,128)(2,1)S(1)}, bf16[16,24,384]{2,1,0:T(8,128)(2,1)S(1)}, u32[]{:S(2)}, u32[]{:S(2)}) collective-permute-start(bf16[16,24,384]{2,1,0:T(8,128)(2,1)S(1)} %all_to_all.15.refs_0_), channel_id=1, source_target_pairs={{0,32},{32,64},{64,96},{96,0},{1,33},{33,65},{65,97},{97,1},{2,34}... | collective-permute-start | bytes 884744 | tf_op jit(solution)/shard_map/ppermute | solution.py:210
  36.2 17.0 %collective-permute-done.3.refs_3_ = bf16[16,24,384]{2,1,0:T(8,128)(2,1)S(1)} collective-permute-done((bf16[16,24,384]{2,1,0:T(8,128)(2,1)S(1)}, bf16[16,24,384]{2,1,0:T(8,128)(2,1)S(1)}, u32[]{:S(2)}, u32[]{:S(2)}) %collective-permute-start.3) | collective-permute-done | bytes 294944 | tf_op jit(solution)/shard_map/ppermute | solution.py:210
  53.2 0.5 collective-permute-start.6
  53.7 0.6 all-to-all-done.own_ref
  54.4 0.0 collective-permute-start
  54.4 2.2 %collective-permute-start.2 = (bf16[16,24,384]{2,1,0:T(8,128)(2,1)S(1)}, bf16[16,24,384]{2,1,0:T(8,128)(2,1)S(1)}, u32[]{:S(2)}, u32[]{:S(2)}) collective-permute-start(bf16[16,24,384]{2,1,0:T(8,128)(2,1)S(1)} %all_to_all.15.refs_0_), channel_id=1, source_target_pairs={{0,96},{32,0},{64,32},{96,64},{1,97},{33,1},{65,33},{97,65},{2,98}... | collective-permute-start | bytes 884744 | tf_op jit(solution)/shard_map/ppermute | solution.py:210
  56.5 0.0 collective-permute-start.5
  56.5 0.0 collective-permute-done.1.refs_1_
  56.5 1.4 %collective-permute-start.4 = (bf16[16,24,384]{2,1,0:T(8,128)(2,1)S(1)}, bf16[16,24,384]{2,1,0:T(8,128)(2,1)S(1)}, u32[]{:S(2)}, u32[]{:S(2)}) collective-permute-start(bf16[16,24,384]{2,1,0:T(8,128)(2,1)S(1)} %collective-permute-done.1.refs_1_), channel_id=1, source_target_pairs={{0,32},{32,64},{64,96},{96,0},{1,33},{33,65},{65,97},{97,1},{2,34}... | collective-permute-start | bytes 884744 | tf_op jit(solution)/shard_map/ppermute | solution.py:210
  57.9 5.2 %collective-permute-done.6.refs_6_ = bf16[16,24,384]{2,1,0:T(8,128)(2,1)S(1)} collective-permute-done((bf16[16,24,384]{2,1,0:T(8,128)(2,1)S(1)}, bf16[16,24,384]{2,1,0:T(8,128)(2,1)S(1)}, u32[]{:S(2)}, u32[]{:S(2)}) %collective-permute-start.6) | collective-permute-done | bytes 294944 | tf_op jit(solution)/shard_map/ppermute | solution.py:210
  63.1 0.8 collective-permute-start.7
  64.6 0.0 copy-start.2
  64.6 0.0 copy-start.3
  64.6 0.0 copy-start.4
  64.6 0.0 copy-start.5
  64.6 0.0 copy-start.6
  64.6 4.8 %collective-permute-done.2.refs_0_.refs_2_ = bf16[16,24,384]{2,1,0:T(8,128)(2,1)S(1)} collective-permute-done((bf16[16,24,384]{2,1,0:T(8,128)(2,1)S(1)}, bf16[16,24,384]{2,1,0:T(8,128)(2,1)S(1)}, u32[]{:S(2)}, u32[]{:S(2)}) %collective-permute-start.2) | collective-permute-done | bytes 294944 | tf_op jit(solution)/shard_map/ppermute | solution.py:210
  69.4 0.0 collective-permute-done.5.refs_1_.refs_5_
  69.4 2.6 %collective-permute-done.4.refs_2_.refs_4_ = bf16[16,24,384]{2,1,0:T(8,128)(2,1)S(1)} collective-permute-done((bf16[16,24,384]{2,1,0:T(8,128)(2,1)S(1)}, bf16[16,24,384]{2,1,0:T(8,128)(2,1)S(1)}, u32[]{:S(2)}, u32[]{:S(2)}) %collective-permute-start.4) | collective-permute-done | bytes 294944 | tf_op jit(solution)/shard_map/ppermute | solution.py:210
  72.0 1.5 %collective-permute-done.7.refs_3_.refs_7_ = bf16[16,24,384]{2,1,0:T(8,128)(2,1)S(1)} collective-permute-done((bf16[16,24,384]{2,1,0:T(8,128)(2,1)S(1)}, bf16[16,24,384]{2,1,0:T(8,128)(2,1)S(1)}, u32[]{:S(2)}, u32[]{:S(2)}) %collective-permute-start.7) | collective-permute-done | bytes 294944 | tf_op jit(solution)/shard_map/ppermute | solution.py:210
  73.5 0.0 collective-permute-done.other_ref
  73.5 0.0 copy-done.2
  73.5 0.0 copy-done.3
  73.5 0.0 copy-done.4
  73.6 0.0 copy-done.5
  73.6 0.0 copy-done.6
  73.6 19.9 %attend.1 = bf16[2,8,3,48,128]{4,3,2,1,0:T(8,128)(2,1)S(1)} custom-call(s32[1]{0:T(128)S(6)} %copy.14.length_ref, bf16[16,3,48,128]{3,2,1,0:T(8,128)(2,1)S(1)} %all-to-all-done.own_ref, bf16[16,3,48,128]{3,2,1,0:T(8,128)(2,1)S(1)} %collective-permute-done.other_ref, bf16[16,24,384]{2,1,0:T(8,128)(2,1)S(1)} %all_to_all.15.refs_0_, ...), custom_call_target="tpu_custom_call" | custom-call | flops 2500000000 | bytes 4000000 | tf_op jit(solution)/shard_map/attend/pallas_call | solution.py:186
  93.5 0.1 collective-permute-start.8
  93.6 1.6 %collective-permute-done.8 = bf16[8,3,48,128]{3,2,1,0:T(8,128)(2,1)S(1)} collective-permute-done((bf16[8,3,48,128]{3,2,1,0:T(8,128)(2,1)S(1)}, bf16[8,3,48,128]{3,2,1,0:T(8,128)(2,1)S(1)}, u32[]{:S(2)}, u32[]{:S(2)}) %collective-permute-start.8) | collective-permute-done | bytes 294944 | tf_op jit(solution)/shard_map/ppermute | solution.py:210
  95.2 0.1 pad_maximum_fusion
  95.3 29.6 %all_to_all.16 = bf16[16,3,48,128]{3,2,1,0:T(8,128)(2,1)S(1)} all-to-all(bf16[16,3,48,128]{3,2,1,0:T(8,128)(2,1)S(1)} %bitcast.17), channel_id=1, replica_groups=mesh['z_lo'=2,'x'=4,'core'=2,'y'=4,'z_hi'=4] {'y','z_hi'}, dimensions={0} | all-to-all | bytes 1179648 | tf_op jit(solution)/shard_map/all_to_all | solution.py:238
  124.9 0.8 copy.15
  (4 shorter events, 0.1 us)
Async XLA Ops:
  0.8 0.7 copy-start.1
  1.5 1.1 copy-start
  30.0 24.4 %all-to-all-start = ((bf16[16,3,48,128]{3,2,1,0:T(8,128)(2,1)}), bf16[16,3,48,128]{3,2,1,0:T(8,128)(2,1)S(1)}, u32[]{:S(2)}, u32[]{:S(2)}) async-start(bf16[16,3,48,128]{3,2,1,0:T(8,128)(2,1)} %bitcast.1), calls=%async_computation | async-start | bytes 1179648 | tf_op jit(solution)/shard_map/all_to_all | solution.py:220
  33.6 19.6 %collective-permute-start.3 = (bf16[16,24,384]{2,1,0:T(8,128)(2,1)S(1)}, bf16[16,24,384]{2,1,0:T(8,128)(2,1)S(1)}, u32[]{:S(2)}, u32[]{:S(2)}) collective-permute-start(bf16[16,24,384]{2,1,0:T(8,128)(2,1)S(1)} %all_to_all.15.refs_0_), channel_id=1, source_target_pairs={{0,128},{128,0},{1,129},{129,1},{2,130},{130,2},{3,131},{131,3},{4... | collective-permute-start | bytes 884744 | tf_op jit(solution)/shard_map/ppermute | solution.py:210
  34.7 21.8 %collective-permute-start.1 = (bf16[16,24,384]{2,1,0:T(8,128)(2,1)S(1)}, bf16[16,24,384]{2,1,0:T(8,128)(2,1)S(1)}, u32[]{:S(2)}, u32[]{:S(2)}) collective-permute-start(bf16[16,24,384]{2,1,0:T(8,128)(2,1)S(1)} %all_to_all.15.refs_0_), channel_id=1, source_target_pairs={{0,32},{32,64},{64,96},{96,0},{1,33},{33,65},{65,97},{97,1},{2,34}... | collective-permute-start | bytes 884744 | tf_op jit(solution)/shard_map/ppermute | solution.py:210
  53.2 9.9 %collective-permute-start.6 = (bf16[16,24,384]{2,1,0:T(8,128)(2,1)S(1)}, bf16[16,24,384]{2,1,0:T(8,128)(2,1)S(1)}, u32[]{:S(2)}, u32[]{:S(2)}) collective-permute-start(bf16[16,24,384]{2,1,0:T(8,128)(2,1)S(1)} %collective-permute-done.3.refs_3_), channel_id=1, source_target_pairs={{0,96},{32,0},{64,32},{96,64},{1,97},{33,1},{65,33},{97,65},{2,98}... | collective-permute-start | bytes 884744 | tf_op jit(solution)/shard_map/ppermute | solution.py:210
  54.4 19.2 %collective-permute-start = (bf16[16,3,48,128]{3,2,1,0:T(8,128)(2,1)S(1)}, bf16[16,3,48,128]{3,2,1,0:T(8,128)(2,1)S(1)}, u32[]{:S(2)}, u32[]{:S(2)}) collective-permute-start(bf16[16,3,48,128]{3,2,1,0:T(8,128)(2,1)S(1)} %all-to-all-done.own_ref), channel_id=1, source_target_pairs={{0,16},{16,0},{1,17},{17,1},{2,18},{18,2},{3,19},{19,3},{4,20},{20... | collective-permute-start | bytes 1769480 | tf_op jit(solution)/shard_map/ppermute | solution.py:210
  54.4 15.1 %collective-permute-start.2 = (bf16[16,24,384]{2,1,0:T(8,128)(2,1)S(1)}, bf16[16,24,384]{2,1,0:T(8,128)(2,1)S(1)}, u32[]{:S(2)}, u32[]{:S(2)}) collective-permute-start(bf16[16,24,384]{2,1,0:T(8,128)(2,1)S(1)} %all_to_all.15.refs_0_), channel_id=1, source_target_pairs={{0,96},{32,0},{64,32},{96,64},{1,97},{33,1},{65,33},{97,65},{2,98}... | collective-permute-start | bytes 884744 | tf_op jit(solution)/shard_map/ppermute | solution.py:210
  56.5 12.9 %collective-permute-start.5 = (bf16[16,24,384]{2,1,0:T(8,128)(2,1)S(1)}, bf16[16,24,384]{2,1,0:T(8,128)(2,1)S(1)}, u32[]{:S(2)}, u32[]{:S(2)}) collective-permute-start(bf16[16,24,384]{2,1,0:T(8,128)(2,1)S(1)} %collective-permute-done.3.refs_3_), channel_id=1, source_target_pairs={{0,32},{32,64},{64,96},{96,0},{1,33},{33,65},{65,97},{97,1},{2,34}... | collective-permute-start | bytes 884744 | tf_op jit(solution)/shard_map/ppermute | solution.py:210
  56.5 15.5 %collective-permute-start.4 = (bf16[16,24,384]{2,1,0:T(8,128)(2,1)S(1)}, bf16[16,24,384]{2,1,0:T(8,128)(2,1)S(1)}, u32[]{:S(2)}, u32[]{:S(2)}) collective-permute-start(bf16[16,24,384]{2,1,0:T(8,128)(2,1)S(1)} %collective-permute-done.1.refs_1_), channel_id=1, source_target_pairs={{0,32},{32,64},{64,96},{96,0},{1,33},{33,65},{65,97},{97,1},{2,34}... | collective-permute-start | bytes 884744 | tf_op jit(solution)/shard_map/ppermute | solution.py:210
  63.1 10.4 %collective-permute-start.7 = (bf16[16,24,384]{2,1,0:T(8,128)(2,1)S(1)}, bf16[16,24,384]{2,1,0:T(8,128)(2,1)S(1)}, u32[]{:S(2)}, u32[]{:S(2)}) collective-permute-start(bf16[16,24,384]{2,1,0:T(8,128)(2,1)S(1)} %collective-permute-done.6.refs_6_), channel_id=1, source_target_pairs={{0,96},{32,0},{64,32},{96,64},{1,97},{33,1},{65,33},{97,65},{2,98}... | collective-permute-start | bytes 884744 | tf_op jit(solution)/shard_map/ppermute | solution.py:210
  64.6 9.0 %copy-start.2 = (bf16[128,128]{1,0:T(8,128)(2,1)S(1)}, bf16[128,128]{1,0:T(8,128)(2,1)}, u32[]{:S(2)}) copy-start(bf16[128,128]{1,0:T(8,128)(2,1)} %refs_8_.1) | copy-start | bytes 98308
  64.6 8.9 %copy-start.3 = (bf16[128,128]{1,0:T(8,128)(2,1)S(1)}, bf16[128,128]{1,0:T(8,128)(2,1)}, u32[]{:S(2)}) copy-start(bf16[128,128]{1,0:T(8,128)(2,1)} %refs_9_.1) | copy-start | bytes 98308
  64.6 8.9 %copy-start.4 = (bf16[128,128]{1,0:T(8,128)(2,1)S(1)}, bf16[128,128]{1,0:T(8,128)(2,1)}, u32[]{:S(2)}) copy-start(bf16[128,128]{1,0:T(8,128)(2,1)} %refs_10_.1) | copy-start | bytes 98308
  64.6 8.9 %copy-start.5 = (bf16[128,128]{1,0:T(8,128)(2,1)S(1)}, bf16[128,128]{1,0:T(8,128)(2,1)}, u32[]{:S(2)}) copy-start(bf16[128,128]{1,0:T(8,128)(2,1)} %refs_11_.1) | copy-start | bytes 98308
  64.6 8.9 %copy-start.6 = (bf16[128,128]{1,0:T(8,128)(2,1)S(1)}, bf16[128,128]{1,0:T(8,128)(2,1)}, u32[]{:S(2)}) copy-start(bf16[128,128]{1,0:T(8,128)(2,1)} %refs_12_.1) | copy-start | bytes 98308
  93.5 1.7 %collective-permute-start.8 = (bf16[8,3,48,128]{3,2,1,0:T(8,128)(2,1)S(1)}, bf16[8,3,48,128]{3,2,1,0:T(8,128)(2,1)S(1)}, u32[]{:S(2)}, u32[]{:S(2)}) collective-permute-start(bf16[8,3,48,128]{3,2,1,0:T(8,128)(2,1)S(1)} %slice_bitcast_fusion), channel_id=1, source_target_pairs={{0,16},{16,0},{1,17},{17,1},{2,18},{18,2},{3,19},{19,3},{4,20},{20... | collective-permute-start | bytes 884744 | tf_op jit(solution)/shard_map/ppermute | solution.py:210

commit v3 on v2

v3 whole, which is shorter than its diff:
```python
import functools
import jax
import jax.numpy as jnp
from jax import lax
from jax.experimental import pallas as pl
from jax.experimental.pallas import tpu as pltpu
from jax.sharding import Mesh, PartitionSpec as P

epsilon = 1e-05
bf16, f32 = jnp.bfloat16, jnp.float32


def contract(a, b, da, db):
    return lax.dot_general(a, b, (((da,), (db,)), ((), ())), preferred_element_type=f32)


def prepare(pair_hbm, gain_ref, w_ref, normed_ref, bias_ref, pair_ref, sems, wide_ref, *, step):
    rows, cols, channels = pair_ref.shape
    heads = w_ref.shape[0]
    half = cols // 2
    lanes = wide_ref.shape[1]
    fetches = [
        pltpu.make_async_copy(pair_hbm.at[pl.ds(g * step, step)], pair_ref.at[pl.ds(g * step, step)], sems.at[g])
        for g in range(rows // step)
    ]
    for fetch in fetches:
        fetch.start()
    gain = gain_ref[...]
    slots = 2 * heads
    mine = lax.axis_index("z_lo") * lax.axis_size("x") + lax.axis_index("x")

    def segment(count):
        slot = lax.broadcasted_iota(jnp.int32, (count, lanes), 1) // rows
        return lax.rem(slot + slots - mine, slots)

    own_head = lax.rem(segment(heads), heads) == lax.broadcasted_iota(jnp.int32, (heads, lanes), 0)
    wide_ref[...] = contract(w_ref[...], jnp.where(own_head, 1.0, 0.0).astype(bf16), 0, 0).astype(bf16)
    first = segment(half) < heads
    lane_j = lax.rem(lax.broadcasted_iota(jnp.int32, (half, lanes), 1), rows)
    acc = jnp.zeros((half, lanes), f32)
    for g, fetch in enumerate(fetches):
        fetch.wait()
        start = g * step
        x = pair_ref[pl.ds(start, step)].reshape(step * cols, channels).astype(f32)
        centred = x - jnp.mean(x, -1, keepdims=True)
        spread = jnp.mean(centred * centred, -1, keepdims=True)
        normed = (centred * lax.rsqrt(spread + epsilon) * gain).astype(bf16)
        normed_ref[pl.ds(start, step)] = normed.reshape(step, cols, channels)
        wide = contract(normed, wide_ref[...], 1, 0)
        for t in range(step):
            one = wide[t * cols : (t + 1) * cols]
            both = jnp.where(first, one[:half], one[half:])
            acc = jnp.where(lane_j == start + t, both, acc)
    bias = acc.astype(bf16)
    for c in range(bias_ref.shape[0]):
        bias_ref[c] = bias


def gate(*refs):
    refs[-1][...] = jnp.zeros_like(refs[-1])


def attend(length_ref, own_hbm, other_hbm, *refs, heads, scale, slots):
    parts_hbm, weights_hbm, refs = refs[:slots], refs[slots : slots + 5], refs[slots + 6 :]
    out_ref, weights, sems, parts, part_sems, both, both_sems = refs[:7]
    table = refs[7]
    keys_of, values_of, queries_of, gates_of, gated_of, scores_of = [refs[n : n + 2] for n in range(8, 20, 2)]
    _, blocks, each, width, channels = both.shape
    half = width // 2
    head = channels // heads
    keys, queries = blocks * width, slots * width
    core, x, z = lax.axis_index("core"), lax.axis_index("x"), lax.axis_index("z_lo")
    along = lax.axis_size("x")
    places = [zz * along + lax.rem(x + by, along) for zz, by in order_of_slots(z, along)]
    fetches = [pltpu.make_async_copy(p, parts.at[q], part_sems.at[n]) for n, (p, q) in enumerate(zip(parts_hbm, places))]
    later = [pltpu.make_async_copy(w, weights.at[n], sems.at[n]) for n, w in enumerate(weights_hbm)]
    later += [pltpu.make_async_copy(r, both.at[n], both_sems.at[n]) for n, r in enumerate((own_hbm, other_hbm))]
    for copy in fetches + later:
        copy.start()
    length = length_ref[0]
    base = (lax.axis_index("y") * lax.axis_size("z_hi") + lax.axis_index("z_hi")) * each
    own_base = (2 * (z * along + x) + core) * (each * blocks) + base
    other_base = (2 * (z * along + x) + 1 - core) * (each * blocks) + base
    for ref in values_of:
        ref[:, head:] = jnp.ones_like(ref[:, head:])
    for copy in fetches:
        copy.wait()
    place = lax.broadcasted_iota(jnp.int32, (half, 128), 1)

    def build(c, carry):
        pieces = [parts[q, c].astype(f32) for q in range(slots)]
        for kh in range(2):
            start = pl.multiple_of(c * width + kh * half, 8)
            valid = start + lax.broadcasted_iota(jnp.int32, (half, 128), 0) < length
            for h in range(heads):
                columns = []
                for at in range(0, queries, 128):
                    inside = range(at // width, -(-(at + 128) // width))
                    value = None
                    for p in inside:
                        new = pieces[(p - kh * heads - h) % slots][:, at : at + 128]
                        value = new if value is None else jnp.where(place >= p * width - at, new, value)
                    columns.append(value)
                if kh == 1:
                    turned = [pltpu.roll(v, 64, 1) for v in columns]
                    columns = [jnp.where(place < 64, turned[(n + 1) % 3], turned[(n + 2) % 3]) for n in range(3)]
                for n, value in enumerate(columns):
                    table[h, pl.ds(start, half), n * 128 : (n + 1) * 128] = jnp.where(valid, value, -1e30)
        return carry

    lax.fori_loop(0, blocks, build, 0)
    for copy in later:
        copy.wait()
    chunk = keys // 2
    steps = keys // chunk
    wq, wk, wo = weights[0], weights[1], weights[4]
    wv = weights[2].T
    wg = weights[3].T
    lane = lax.broadcasted_iota(jnp.int32, (width, channels), 1)
    of_head = [(lane >= h * head) & (lane < (h + 1) * head) for h in range(heads)]

    def cells(n, chosen):
        side, t = n // each, lax.rem(n, each)
        return jnp.concatenate([both[side, c, t] for c in chosen], axis=0)

    def project_keys(n, to):
        keys_of[to][...] = contract(cells(n, range(blocks)), wk, 1, 0).astype(bf16)

    def project_values(n, to):
        value = contract(wv, cells(n, range(blocks)), 1, 1).astype(bf16)
        for h in range(heads):
            values_of[to][h, :head] = value[h * head : (h + 1) * head]

    def project_queries(n, to):
        asked = cells(n, [2 * q + core for q in range(slots)])
        query = (contract(asked, wq, 1, 0) * scale).astype(bf16)
        for h in range(heads):
            for p in range(slots):
                q = (p - h) % slots
                block = query[q * width : (q + 1) * width]
                queries_of[to][h, p * width : (p + 1) * width] = jnp.where(of_head[h], block, jnp.zeros_like(block))

    def project_gates(n, to):
        asked = cells(n, [2 * q + core for q in range(slots)])
        gates_of[to][...] = jax.nn.sigmoid(contract(wg, asked, 1, 1)).astype(bf16).astype(f32)

    def score(at, h, k, top):
        part = pl.ds(k * chunk, chunk)
        scores = contract(keys_of[at][part], queries_of[at][h], 1, 1) + table[h, part]
        scores_of[h % 2][part] = scores
        best = jnp.max(scores.reshape(chunk // 8, 8, queries), 0)
        return best if top is None else jnp.maximum(top, best)

    def blend(at, h, k, highest, sofar):
        exponent = jnp.exp(scores_of[h % 2][pl.ds(k * chunk, chunk)] - highest).astype(bf16)
        more = contract(values_of[at][h, :, k * chunk : (k + 1) * chunk], exponent, 1, 0)
        return more if sofar is None else sofar + more

    def one_row(n, at, top):
        following = jnp.minimum(n + 1, 2 * each - 1)
        for h in range(heads):
            highest = jnp.max(top, 0, keepdims=True)
            top, total = None, None
            for k in range(steps):
                if h + 1 < heads:
                    top = score(at, h + 1, k, top)
                else:
                    top = score(1 - at, 0, k, top)
                total = blend(at, h, k, highest, total)
                if h == 0 and k == 0:
                    project_keys(following, 1 - at)
                if h == 0 and k == 1:
                    project_queries(following, 1 - at)
                if h == 1 and k == 0:
                    project_values(following, 1 - at)
                if h == 2 and k == 0:
                    project_gates(following, 1 - at)
            blended = total[:head] / total[head : head + 1]
            if h > 0:
                blended = jnp.concatenate([blended[:, h * width :], blended[:, : h * width]], axis=1)
            part = slice(h * head, (h + 1) * head)
            gated_of[at][part] = (gates_of[at][part] * blended).astype(bf16)
        update = contract(gated_of[at][...], wo, 0, 0)
        side, t = n // each, lax.rem(n, each)
        row_ok = jnp.where(side == 0, own_base, other_base) + t < length
        row = lax.broadcasted_iota(jnp.int32, (width, channels), 0)
        for q in range(slots):
            ok = (row + (2 * q + core) * width < length) & row_ok
            piece = update[q * width : (q + 1) * width]
            out_ref[side, q, t] = jnp.where(ok, piece, 0.0).astype(bf16)
        return top

    for first in (project_keys, project_queries, project_values, project_gates):
        first(0, 0)
    top = None
    for k in range(steps):
        top = score(0, 0, k, top)
    lax.fori_loop(0, each, lambda n, top: one_row(2 * n + 1, 1, one_row(2 * n, 0, top)), top)


ROW, COL = ("z_lo", "x", "core"), ("y", "z_hi")
ALL_VMEM = 67043328
VMEM = pl.BlockSpec(memory_space=pltpu.VMEM)
HBM = pl.BlockSpec(memory_space=pltpu.HBM)
SMEM = pl.BlockSpec(memory_space=pltpu.SMEM)


def run_prepare(pair, ln_gain, w_bias, across):
    tile_rows, tile_cols, channels = pair.shape
    heads = w_bias.shape[1]
    half = tile_cols // 2
    lanes = 2 * heads * tile_rows
    step = 12
    return pl.pallas_call(
        functools.partial(prepare, step=step),
        out_shape=(
            jax.ShapeDtypeStruct(pair.shape, bf16),
            jax.ShapeDtypeStruct((across, half, lanes), bf16),
        ),
        in_specs=[HBM, pl.BlockSpec(), pl.BlockSpec()],
        out_specs=(VMEM, VMEM),
        scratch_shapes=[
            pltpu.VMEM(pair.shape, bf16),
            pltpu.SemaphoreType.DMA((tile_rows // step,)),
            pltpu.VMEM((channels, lanes), bf16),
        ],
        compiler_params=pltpu.CompilerParams(vmem_limit_bytes=ALL_VMEM),
        name="prepare",
    )(pair, ln_gain.reshape(1, channels), w_bias.T)


def order_of_slots(z, along):
    near = [(z, 0), (z, along - 1), (z, 1), (1 - z, 0)]
    return near + [(z, along - 2), (1 - z, along - 1), (1 - z, 1), (1 - z, 2)]


def run_gate(arrays):
    return pl.pallas_call(
        gate,
        out_shape=jax.ShapeDtypeStruct((8, 128), f32),
        in_specs=[HBM] * len(arrays),
        out_specs=VMEM,
        compiler_params=pltpu.CompilerParams(vmem_limit_bytes=1 << 20),
        name="gate",
    )(*arrays)


def run_attend(length, own, other, parts, weights, passed, heads):
    blocks, each, width, channels = own.shape
    slots = len(parts)
    keys, queries = blocks * width, slots * width
    head = channels // heads
    return pl.pallas_call(
        functools.partial(attend, heads=heads, scale=head**-0.5, slots=slots),
        out_shape=jax.ShapeDtypeStruct((2, slots, each, width, channels), bf16),
        in_specs=[SMEM] + [HBM] * (slots + 8),
        out_specs=VMEM,
        scratch_shapes=[
            pltpu.VMEM((5, channels, channels), bf16),
            pltpu.SemaphoreType.DMA((5,)),
            pltpu.VMEM((slots, *parts[0].shape), bf16),
            pltpu.SemaphoreType.DMA((slots,)),
            pltpu.VMEM((2, *own.shape), bf16),
            pltpu.SemaphoreType.DMA((2,)),
            pltpu.VMEM((heads, keys, queries), f32),
        ]
        + [pltpu.VMEM((keys, channels), bf16)] * 2
        + [pltpu.VMEM((heads, head + 16, keys), bf16)] * 2
        + [pltpu.VMEM((heads, queries, channels), bf16)] * 2
        + [pltpu.VMEM((channels, queries), f32)] * 2
        + [pltpu.VMEM((channels, queries), bf16)] * 2
        + [pltpu.VMEM((keys, queries), f32)] * 2,
        compiler_params=pltpu.CompilerParams(vmem_limit_bytes=66060288),
        cost_estimate=pl.CostEstimate(flops=2_500_000_000, transcendentals=7_000_000, bytes_accessed=4_000_000),
        name="attend",
    )(length, own, other, *parts, *weights, passed)


def shifted(value, axis, by):
    n = lax.axis_size(axis)
    return lax.ppermute(value, axis, [(k, (k + by) % n) for k in range(n)])


def per_device_inner(pair, ln_gain, w_query, w_key, w_value, w_gate, w_bias, w_out, valid_length):
    tile_rows, tile_cols, channels = pair.shape
    heads = w_bias.shape[1]
    across = lax.axis_size(COL)
    each = tile_rows // across
    weights = (w_query, w_key, w_value, w_gate, w_out)
    normed, bias = run_prepare(pair, ln_gain, w_bias, across)
    mine = lax.all_to_all(bias, COL, 0, 0, tiled=True)
    own = lax.all_to_all(normed.reshape(across, each, tile_cols, channels), COL, 0, 0, tiled=True)
    below = shifted(mine, "z_lo", 1)
    left = shifted(mine, "x", 1)
    right = shifted(mine, "x", -1)
    below_left = shifted(below, "x", 1)
    below_right = shifted(below, "x", -1)
    far = shifted(left, "x", 1)
    below_far = shifted(below_right, "x", -1)
    passed = run_gate([right, below_left, far, below_far])
    other = shifted(own, "core", 1)
    parts = [mine, left, right, below, far, below_left, below_right, below_far]
    out = run_attend(valid_length, own, other, parts, weights, passed, heads)
    theirs = shifted(out[1], "core", 1)
    core = lax.axis_index("core")
    even = jnp.where(core == 0, out[0], theirs)
    odd = jnp.where(core == 0, theirs, out[0])
    update = jnp.stack([even, odd], axis=1).reshape(across, each, tile_cols, channels)
    update = lax.all_to_all(update, COL, 0, 0, tiled=True)
    return update.reshape(tile_rows, tile_cols, channels)


def solution(mesh):
    fine = Mesh(mesh.devices.reshape(2, 4, 2, 4, 4), ROW + COL)
    placed = (P(ROW, COL, None), P(), P(), P(), P(), P(), P(), P(), P())
    return jax.shard_map(per_device_inner, mesh=fine, in_specs=placed, out_specs=P(ROW, COL, None), check_vma=False)
```

time: 127 us -> 126 us (level)
  Pallas kernels: 22.4 us -> 20.7 us
    pallas_call x1, Pallas kernels: 19.9 us -> 15.9 us  [run_attend(): pl.pallas_call(functools.partial(attend, heads=heads, scale=head ** (-0.5...]
    pallas_call x1, Pallas kernels: 2.53 us -> 4.79 us  [run_prepare(): pl.pallas_call(functools.partial(prepare, step=step), out_shape=(jax.Shap...]
    unnamed x16 -> x25, local copies, waits for them, and re-layouts: 3.37 us -> 2.92 us
where the time goes in v3:
time: 126 us; the launch traced here: 125 us
  blocking collectives  54.7 us (43%)
  waiting for transfers between devices  33.3 us (26%)
  Pallas kernels  20.7 us (16%)
  starting transfers between devices  11.2 us (9%)
  local copies, waits for them, and re-layouts  4.01 us (3%)
    ppermute x9, waiting for transfers between devices, shifted(): return lax.ppermute(value, axis, [(k, (k + by) % n) for k in range(n)])  32.7 us
    all_to_all x1, blocking collectives, per_device_inner(): update = lax.all_to_all(update, COL, 0, 0, tiled=True)  29.6 us
    all_to_all x1, blocking collectives, per_device_inner(): mine = lax.all_to_all(bias, COL, 0, 0, tiled=True)  25.2 us
    pallas_call x1, Pallas kernels, run_attend(): pl.pallas_call(functools.partial(attend, heads=heads, scale=head ** (-0.5...  15.9 us
    ppermute x9, starting transfers between devices, shifted(): return lax.ppermute(value, axis, [(k, (k + by) % n) for k in range(n)])  7.59 us
    pallas_call x1, Pallas kernels, run_prepare(): pl.pallas_call(functools.partial(prepare, step=step), out_shape=(jax.Shap...  4.79 us
    all_to_all x1, starting transfers between devices, per_device_inner(): lax.all_to_all(normed.reshape(across, each, tile_cols, channels), COL, 0,...  3.58 us
    unnamed x25, local copies, waits for them, and re-layouts  2.92 us
  transfers between devices with their start and end apart: 10, of which 7 were waited for; matrix products, arithmetic and copies ran while one was open for 0% of the time, Pallas kernels for 0%

profile of v3, /device:TPU:2, one launch (start us, length us, event | category | flops | bytes accessed | tf_op | source)
XLA Modules:
  0.0 124.8 jit_solution(3212518642166522679)
XLA Ops:
  0.0 4.8 %prepare.1 = (bf16[48,48,128]{2,1,0:T(8,128)(2,1)}, bf16[16,24,384]{2,1,0:T(8,128)(2,1)}) custom-call(bf16[48,48,128]{2,1,0:T(8,128)(2,1)} %pair_hbm.1, f32[1,128]{1,0:T(1,128)} %bitcast.20, bf16[4,128]{1,0:T(4,128)(2,1)} %bitcast.19), custom_call_target="tpu_custom_call" | custom-call | tf_op jit(solution)/shard_map/prepare/pallas_call | solution.py:214
  4.8 25.2 %all_to_all.15.refs_0_ = bf16[16,24,384]{2,1,0:T(8,128)(2,1)S(1)} all-to-all(bf16[16,24,384]{2,1,0:T(8,128)(2,1)} %get-tuple-element.8), channel_id=1, replica_groups=mesh['z_lo'=2,'x'=4,'core'=2,'y'=4,'z_hi'=4] {'y','z_hi'}, dimensions={0} | all-to-all | bytes 589824 | tf_op jit(solution)/shard_map/all_to_all | solution.py:291
  30.0 0.0 copy-start.7
  30.0 3.6 %all-to-all-start = ((bf16[16,3,48,128]{3,2,1,0:T(8,128)(2,1)}), bf16[16,3,48,128]{3,2,1,0:T(8,128)(2,1)S(1)}, u32[]{:S(2)}, u32[]{:S(2)}) async-start(bf16[16,3,48,128]{3,2,1,0:T(8,128)(2,1)} %bitcast.2), calls=%async_computation | async-start | bytes 1179648 | tf_op jit(solution)/shard_map/all_to_all | solution.py:292
  33.6 1.1 collective-permute-start.3
  34.7 1.5 %collective-permute-start.1 = (bf16[16,24,384]{2,1,0:T(8,128)(2,1)S(1)}, bf16[16,24,384]{2,1,0:T(8,128)(2,1)S(1)}, u32[]{:S(2)}, u32[]{:S(2)}) collective-permute-start(bf16[16,24,384]{2,1,0:T(8,128)(2,1)S(1)} %all_to_all.15.refs_0_), channel_id=1, source_target_pairs={{0,32},{32,64},{64,96},{96,0},{1,33},{33,65},{65,97},{97,1},{2,34}... | collective-permute-start | bytes 884744 | tf_op jit(solution)/shard_map/ppermute | solution.py:281
  36.1 17.0 %collective-permute-done.3.refs_3_ = bf16[16,24,384]{2,1,0:T(8,128)(2,1)S(1)} collective-permute-done((bf16[16,24,384]{2,1,0:T(8,128)(2,1)S(1)}, bf16[16,24,384]{2,1,0:T(8,128)(2,1)S(1)}, u32[]{:S(2)}, u32[]{:S(2)}) %collective-permute-start.3) | collective-permute-done | bytes 294944 | tf_op jit(solution)/shard_map/ppermute | solution.py:281
  53.2 0.0 copy-start.9
  53.2 0.5 collective-permute-start.6
  53.7 0.6 all-to-all-done.own_hbm
  54.3 0.0 copy-start.5
  54.3 0.0 collective-permute-start
  54.3 0.0 copy-done.7
  54.3 2.3 %collective-permute-start.2 = (bf16[16,24,384]{2,1,0:T(8,128)(2,1)S(1)}, bf16[16,24,384]{2,1,0:T(8,128)(2,1)S(1)}, u32[]{:S(2)}, u32[]{:S(2)}) collective-permute-start(bf16[16,24,384]{2,1,0:T(8,128)(2,1)S(1)} %all_to_all.15.refs_0_), channel_id=1, source_target_pairs={{0,96},{32,0},{64,32},{96,64},{1,97},{33,1},{65,33},{97,65},{2,98}... | collective-permute-start | bytes 884744 | tf_op jit(solution)/shard_map/ppermute | solution.py:281
  56.6 0.0 collective-permute-start.5
  56.6 0.0 collective-permute-done.1.refs_1_
  56.6 0.0 copy-start.10
  56.6 1.3 %collective-permute-start.4 = (bf16[16,24,384]{2,1,0:T(8,128)(2,1)S(1)}, bf16[16,24,384]{2,1,0:T(8,128)(2,1)S(1)}, u32[]{:S(2)}, u32[]{:S(2)}) collective-permute-start(bf16[16,24,384]{2,1,0:T(8,128)(2,1)S(1)} %collective-permute-done.1.refs_1_), channel_id=1, source_target_pairs={{0,32},{32,64},{64,96},{96,0},{1,33},{33,65},{65,97},{97,1},{2,34}... | collective-permute-start | bytes 884744 | tf_op jit(solution)/shard_map/ppermute | solution.py:281
  57.9 5.2 %collective-permute-done.6.refs_6_ = bf16[16,24,384]{2,1,0:T(8,128)(2,1)S(1)} collective-permute-done((bf16[16,24,384]{2,1,0:T(8,128)(2,1)S(1)}, bf16[16,24,384]{2,1,0:T(8,128)(2,1)S(1)}, u32[]{:S(2)}, u32[]{:S(2)}) %collective-permute-start.6) | collective-permute-done | bytes 294944 | tf_op jit(solution)/shard_map/ppermute | solution.py:281
  63.1 0.0 copy-start.11
  63.1 0.8 collective-permute-start.7
  64.5 4.9 %collective-permute-done.2.refs_0_.refs_2_ = bf16[16,24,384]{2,1,0:T(8,128)(2,1)S(1)} collective-permute-done((bf16[16,24,384]{2,1,0:T(8,128)(2,1)S(1)}, bf16[16,24,384]{2,1,0:T(8,128)(2,1)S(1)}, u32[]{:S(2)}, u32[]{:S(2)}) %collective-permute-start.2) | collective-permute-done | bytes 294944 | tf_op jit(solution)/shard_map/ppermute | solution.py:281
  69.4 0.0 copy-start
  69.4 0.0 collective-permute-done.5.refs_1_.refs_5_
  69.4 0.0 copy-start.1
  69.4 2.6 %collective-permute-done.4.refs_2_.refs_4_ = bf16[16,24,384]{2,1,0:T(8,128)(2,1)S(1)} collective-permute-done((bf16[16,24,384]{2,1,0:T(8,128)(2,1)S(1)}, bf16[16,24,384]{2,1,0:T(8,128)(2,1)S(1)}, u32[]{:S(2)}, u32[]{:S(2)}) %collective-permute-start.4) | collective-permute-done | bytes 294944 | tf_op jit(solution)/shard_map/ppermute | solution.py:281
  72.0 0.0 copy-start.2
  72.0 1.5 %collective-permute-done.7.refs_3_.refs_7_ = bf16[16,24,384]{2,1,0:T(8,128)(2,1)S(1)} collective-permute-done((bf16[16,24,384]{2,1,0:T(8,128)(2,1)S(1)}, bf16[16,24,384]{2,1,0:T(8,128)(2,1)S(1)}, u32[]{:S(2)}, u32[]{:S(2)}) %collective-permute-start.7) | collective-permute-done | bytes 294944 | tf_op jit(solution)/shard_map/ppermute | solution.py:281
  73.5 0.0 copy-start.3
  73.5 0.0 copy-done.5
  73.5 0.0 copy-done.10
  73.5 0.0 copy-done.11
  73.5 0.0 copy-done
  73.5 0.0 copy-done.1
  73.5 0.0 copy-done.2
  73.5 0.7 copy-done.3
  74.2 0.0 copy-start.4
  74.2 0.6 copy-done.4
  74.8 0.0 collective-permute-done.other_hbm
  74.8 0.0 copy-done.9
  74.8 0.0 copy-start.8
  74.8 0.8 copy-done.8
  75.6 15.9 %attend.1 = bf16[2,8,3,48,128]{4,3,2,1,0:T(8,128)(2,1)} custom-call(s32[1]{0:T(128)S(6)} %copy.12.length_ref, bf16[16,3,48,128]{3,2,1,0:T(8,128)(2,1)} %copy-done.5, bf16[16,3,48,128]{3,2,1,0:T(8,128)(2,1)} %copy-done.8, bf16[16,24,384]{2,1,0:T(8,128)(2,1)} %copy-done.7, bf16[16,24,384]{2,1,0:T(8,128)(2,1)} %copy-done.10, bf16[16,24,384]{2,1,0:T(8,128)(2,1)} %copy-done, ...), custom_call_target="tpu_custom_call" | custom-call | flops 2500000000 | bytes 4000000 | tf_op jit(solution)/shard_map/attend/pallas_call | solution.py:253
  91.6 0.0 copy-start.6
  91.6 1.0 slice_bitcast_fusion
  92.6 0.1 collective-permute-start.8
  92.7 1.6 %collective-permute-done.8 = bf16[8,3,48,128]{3,2,1,0:T(8,128)(2,1)S(1)} collective-permute-done((bf16[8,3,48,128]{3,2,1,0:T(8,128)(2,1)S(1)}, bf16[8,3,48,128]{3,2,1,0:T(8,128)(2,1)S(1)}, u32[]{:S(2)}, u32[]{:S(2)}) %collective-permute-start.8) | collective-permute-done | bytes 294944 | tf_op jit(solution)/shard_map/ppermute | solution.py:281
  94.3 0.0 copy-done.6
  94.3 0.1 pad_maximum_fusion
  94.4 29.6 %all_to_all.16 = bf16[16,3,48,128]{3,2,1,0:T(8,128)(2,1)S(1)} all-to-all(bf16[16,3,48,128]{3,2,1,0:T(8,128)(2,1)S(1)} %bitcast.17), channel_id=1, replica_groups=mesh['z_lo'=2,'x'=4,'core'=2,'y'=4,'z_hi'=4] {'y','z_hi'}, dimensions={0} | all-to-all | bytes 1179648 | tf_op jit(solution)/shard_map/all_to_all | solution.py:309
  124.0 0.8 copy.13
  (3 shorter events, 0.1 us)
Async XLA Ops:
  30.0 24.4 %copy-start.7 = (bf16[16,24,384]{2,1,0:T(8,128)(2,1)}, bf16[16,24,384]{2,1,0:T(8,128)(2,1)S(1)}, u32[]{:S(2)}) copy-start(bf16[16,24,384]{2,1,0:T(8,128)(2,1)S(1)} %all_to_all.15.refs_0_) | copy-start | bytes 884740
  30.0 24.3 %all-to-all-start = ((bf16[16,3,48,128]{3,2,1,0:T(8,128)(2,1)}), bf16[16,3,48,128]{3,2,1,0:T(8,128)(2,1)S(1)}, u32[]{:S(2)}, u32[]{:S(2)}) async-start(bf16[16,3,48,128]{3,2,1,0:T(8,128)(2,1)} %bitcast.2), calls=%async_computation | async-start | bytes 1179648 | tf_op jit(solution)/shard_map/all_to_all | solution.py:292
  33.6 19.6 %collective-permute-start.3 = (bf16[16,24,384]{2,1,0:T(8,128)(2,1)S(1)}, bf16[16,24,384]{2,1,0:T(8,128)(2,1)S(1)}, u32[]{:S(2)}, u32[]{:S(2)}) collective-permute-start(bf16[16,24,384]{2,1,0:T(8,128)(2,1)S(1)} %all_to_all.15.refs_0_), channel_id=1, source_target_pairs={{0,128},{128,0},{1,129},{129,1},{2,130},{130,2},{3,131},{131,3},{4... | collective-permute-start | bytes 884744 | tf_op jit(solution)/shard_map/ppermute | solution.py:281
  34.7 21.9 %collective-permute-start.1 = (bf16[16,24,384]{2,1,0:T(8,128)(2,1)S(1)}, bf16[16,24,384]{2,1,0:T(8,128)(2,1)S(1)}, u32[]{:S(2)}, u32[]{:S(2)}) collective-permute-start(bf16[16,24,384]{2,1,0:T(8,128)(2,1)S(1)} %all_to_all.15.refs_0_), channel_id=1, source_target_pairs={{0,32},{32,64},{64,96},{96,0},{1,33},{33,65},{65,97},{97,1},{2,34}... | collective-permute-start | bytes 884744 | tf_op jit(solution)/shard_map/ppermute | solution.py:281
  53.2 21.6 %copy-start.9 = (bf16[16,24,384]{2,1,0:T(8,128)(2,1)}, bf16[16,24,384]{2,1,0:T(8,128)(2,1)S(1)}, u32[]{:S(2)}) copy-start(bf16[16,24,384]{2,1,0:T(8,128)(2,1)S(1)} %collective-permute-done.3.refs_3_) | copy-start | bytes 884740
  53.2 9.9 %collective-permute-start.6 = (bf16[16,24,384]{2,1,0:T(8,128)(2,1)S(1)}, bf16[16,24,384]{2,1,0:T(8,128)(2,1)S(1)}, u32[]{:S(2)}, u32[]{:S(2)}) collective-permute-start(bf16[16,24,384]{2,1,0:T(8,128)(2,1)S(1)} %collective-permute-done.3.refs_3_), channel_id=1, source_target_pairs={{0,96},{32,0},{64,32},{96,64},{1,97},{33,1},{65,33},{97,65},{2,98}... | collective-permute-start | bytes 884744 | tf_op jit(solution)/shard_map/ppermute | solution.py:281
  54.3 19.2 %copy-start.5 = (bf16[16,3,48,128]{3,2,1,0:T(8,128)(2,1)}, bf16[16,3,48,128]{3,2,1,0:T(8,128)(2,1)S(1)}, u32[]{:S(2)}) copy-start(bf16[16,3,48,128]{3,2,1,0:T(8,128)(2,1)S(1)} %all-to-all-done.own_hbm) | copy-start | bytes 1769476
  54.3 20.5 %collective-permute-start = (bf16[16,3,48,128]{3,2,1,0:T(8,128)(2,1)S(1)}, bf16[16,3,48,128]{3,2,1,0:T(8,128)(2,1)S(1)}, u32[]{:S(2)}, u32[]{:S(2)}) collective-permute-start(bf16[16,3,48,128]{3,2,1,0:T(8,128)(2,1)S(1)} %all-to-all-done.own_hbm), channel_id=1, source_target_pairs={{0,16},{16,0},{1,17},{17,1},{2,18},{18,2},{3,19},{19,3},{4,20},{20... | collective-permute-start | bytes 1769480 | tf_op jit(solution)/shard_map/ppermute | solution.py:281
  54.3 15.1 %collective-permute-start.2 = (bf16[16,24,384]{2,1,0:T(8,128)(2,1)S(1)}, bf16[16,24,384]{2,1,0:T(8,128)(2,1)S(1)}, u32[]{:S(2)}, u32[]{:S(2)}) collective-permute-start(bf16[16,24,384]{2,1,0:T(8,128)(2,1)S(1)} %all_to_all.15.refs_0_), channel_id=1, source_target_pairs={{0,96},{32,0},{64,32},{96,64},{1,97},{33,1},{65,33},{97,65},{2,98}... | collective-permute-start | bytes 884744 | tf_op jit(solution)/shard_map/ppermute | solution.py:281
  56.6 12.8 %collective-permute-start.5 = (bf16[16,24,384]{2,1,0:T(8,128)(2,1)S(1)}, bf16[16,24,384]{2,1,0:T(8,128)(2,1)S(1)}, u32[]{:S(2)}, u32[]{:S(2)}) collective-permute-start(bf16[16,24,384]{2,1,0:T(8,128)(2,1)S(1)} %collective-permute-done.3.refs_3_), channel_id=1, source_target_pairs={{0,32},{32,64},{64,96},{96,0},{1,33},{33,65},{65,97},{97,1},{2,34}... | collective-permute-start | bytes 884744 | tf_op jit(solution)/shard_map/ppermute | solution.py:281
  56.6 16.9 %copy-start.10 = (bf16[16,24,384]{2,1,0:T(8,128)(2,1)}, bf16[16,24,384]{2,1,0:T(8,128)(2,1)S(1)}, u32[]{:S(2)}) copy-start(bf16[16,24,384]{2,1,0:T(8,128)(2,1)S(1)} %collective-permute-done.1.refs_1_) | copy-start | bytes 884740
  56.6 15.4 %collective-permute-start.4 = (bf16[16,24,384]{2,1,0:T(8,128)(2,1)S(1)}, bf16[16,24,384]{2,1,0:T(8,128)(2,1)S(1)}, u32[]{:S(2)}, u32[]{:S(2)}) collective-permute-start(bf16[16,24,384]{2,1,0:T(8,128)(2,1)S(1)} %collective-permute-done.1.refs_1_), channel_id=1, source_target_pairs={{0,32},{32,64},{64,96},{96,0},{1,33},{33,65},{65,97},{97,1},{2,34}... | collective-permute-start | bytes 884744 | tf_op jit(solution)/shard_map/ppermute | solution.py:281
  63.1 10.4 %copy-start.11 = (bf16[16,24,384]{2,1,0:T(8,128)(2,1)}, bf16[16,24,384]{2,1,0:T(8,128)(2,1)S(1)}, u32[]{:S(2)}) copy-start(bf16[16,24,384]{2,1,0:T(8,128)(2,1)S(1)} %collective-permute-done.6.refs_6_) | copy-start | bytes 884740
  63.1 10.4 %collective-permute-start.7 = (bf16[16,24,384]{2,1,0:T(8,128)(2,1)S(1)}, bf16[16,24,384]{2,1,0:T(8,128)(2,1)S(1)}, u32[]{:S(2)}, u32[]{:S(2)}) collective-permute-start(bf16[16,24,384]{2,1,0:T(8,128)(2,1)S(1)} %collective-permute-done.6.refs_6_), channel_id=1, source_target_pairs={{0,96},{32,0},{64,32},{96,64},{1,97},{33,1},{65,33},{97,65},{2,98}... | collective-permute-start | bytes 884744 | tf_op jit(solution)/shard_map/ppermute | solution.py:281
  69.4 4.1 %copy-start = (bf16[16,24,384]{2,1,0:T(8,128)(2,1)}, bf16[16,24,384]{2,1,0:T(8,128)(2,1)S(1)}, u32[]{:S(2)}) copy-start(bf16[16,24,384]{2,1,0:T(8,128)(2,1)S(1)} %collective-permute-done.2.refs_0_.refs_2_) | copy-start | bytes 884740
  69.4 4.1 %copy-start.1 = (bf16[16,24,384]{2,1,0:T(8,128)(2,1)}, bf16[16,24,384]{2,1,0:T(8,128)(2,1)S(1)}, u32[]{:S(2)}) copy-start(bf16[16,24,384]{2,1,0:T(8,128)(2,1)S(1)} %collective-permute-done.5.refs_1_.refs_5_) | copy-start | bytes 884740
  72.0 1.6 %copy-start.2 = (bf16[16,24,384]{2,1,0:T(8,128)(2,1)}, bf16[16,24,384]{2,1,0:T(8,128)(2,1)S(1)}, u32[]{:S(2)}) copy-start(bf16[16,24,384]{2,1,0:T(8,128)(2,1)S(1)} %collective-permute-done.4.refs_2_.refs_4_) | copy-start | bytes 884740
  73.5 0.7 copy-start.3
  74.2 0.6 copy-start.4
  74.8 0.8 copy-start.8
  91.6 2.7 %copy-start.6 = (bf16[2,8,3,48,128]{4,3,2,1,0:T(8,128)(2,1)S(1)}, bf16[2,8,3,48,128]{4,3,2,1,0:T(8,128)(2,1)}, u32[]{:S(2)}) copy-start(bf16[2,8,3,48,128]{4,3,2,1,0:T(8,128)(2,1)} %attend.1) | copy-start | bytes 1769476
  92.6 1.7 %collective-permute-start.8 = (bf16[8,3,48,128]{3,2,1,0:T(8,128)(2,1)S(1)}, bf16[8,3,48,128]{3,2,1,0:T(8,128)(2,1)S(1)}, u32[]{:S(2)}, u32[]{:S(2)}) collective-permute-start(bf16[8,3,48,128]{3,2,1,0:T(8,128)(2,1)S(1)} %slice_bitcast_fusion), channel_id=1, source_target_pairs={{0,16},{16,0},{1,17},{17,1},{2,18},{18,2},{3,19},{19,3},{4,20},{20... | collective-permute-start | bytes 884744 | tf_op jit(solution)/shard_map/ppermute | solution.py:281

commit v4 on v3

--- a/solution.py
+++ b/solution.py
@@ -14,7 +14,8 @@
     return lax.dot_general(a, b, (((da,), (db,)), ((), ())), preferred_element_type=f32)
 
 
-def prepare(pair_hbm, gain_ref, w_ref, normed_ref, bias_ref, pair_ref, sems, wide_ref, *, step):
+def prepare(pair_hbm, gain_ref, w_ref, normed_hbm, bias_hbm, *refs, step):
+    pair_ref, sems, normed_ref, normed_sems, bias_ref, bias_sems, wide_ref = refs
     rows, cols, channels = pair_ref.shape
     heads = w_ref.shape[0]
     half = cols // 2
@@ -38,6 +39,7 @@
     first = segment(half) < heads
     lane_j = lax.rem(lax.broadcasted_iota(jnp.int32, (half, lanes), 1), rows)
     acc = jnp.zeros((half, lanes), f32)
+    stores = []
     for g, fetch in enumerate(fetches):
         fetch.wait()
         start = g * step
@@ -46,14 +48,20 @@
         spread = jnp.mean(centred * centred, -1, keepdims=True)
         normed = (centred * lax.rsqrt(spread + epsilon) * gain).astype(bf16)
         normed_ref[pl.ds(start, step)] = normed.reshape(step, cols, channels)
+        part = pl.ds(start, step)
+        stores.append(pltpu.make_async_copy(normed_ref.at[part], normed_hbm.at[part], normed_sems.at[g]))
+        stores[-1].start()
         wide = contract(normed, wide_ref[...], 1, 0)
         for t in range(step):
             one = wide[t * cols : (t + 1) * cols]
             both = jnp.where(first, one[:half], one[half:])
             acc = jnp.where(lane_j == start + t, both, acc)
-    bias = acc.astype(bf16)
-    for c in range(bias_ref.shape[0]):
-        bias_ref[c] = bias
+    bias_ref[...] = acc.astype(bf16)
+    for c in range(bias_hbm.shape[0]):
+        stores.append(pltpu.make_async_copy(bias_ref, bias_hbm.at[c], bias_sems.at[c]))
+        stores[-1].start()
+    for store in stores:
+        store.wait()
 
 
 def gate(*refs):
@@ -218,10 +226,14 @@
             jax.ShapeDtypeStruct((across, half, lanes), bf16),
         ),
         in_specs=[HBM, pl.BlockSpec(), pl.BlockSpec()],
-        out_specs=(VMEM, VMEM),
+        out_specs=(HBM, HBM),
         scratch_shapes=[
             pltpu.VMEM(pair.shape, bf16),
             pltpu.SemaphoreType.DMA((tile_rows // step,)),
+            pltpu.VMEM(pair.shape, bf16),
+            pltpu.SemaphoreType.DMA((tile_rows // step,)),
+            pltpu.VMEM((half, lanes), bf16),
+            pltpu.SemaphoreType.DMA((across,)),
             pltpu.VMEM((channels, lanes), bf16),
         ],
         compiler_params=pltpu.CompilerParams(vmem_limit_bytes=ALL_VMEM),
@@ -270,7 +282,7 @@
         + [pltpu.VMEM((channels, queries), f32)] * 2
         + [pltpu.VMEM((channels, queries), bf16)] * 2
         + [pltpu.VMEM((keys, queries), f32)] * 2,
-        compiler_params=pltpu.CompilerParams(vmem_limit_bytes=66060288),
+        compiler_params=pltpu.CompilerParams(vmem_limit_bytes=24 << 20),
         cost_estimate=pl.CostEstimate(flops=2_500_000_000, transcendentals=7_000_000, bytes_accessed=4_000_000),
         name="attend",
     )(length, own, other, *parts, *weights, passed)
@@ -286,7 +298,7 @@
     heads = w_bias.shape[1]
     across = lax.axis_size(COL)
     each = tile_rows // across
-    weights = (w_query, w_key, w_value, w_gate, w_out)
+    weights = [pltpu.with_memory_space_constraint(w, pltpu.HBM) for w in (w_query, w_key, w_value, w_gate, w_out)]
     normed, bias = run_prepare(pair, ln_gain, w_bias, across)
     mine = lax.all_to_all(bias, COL, 0, 0, tiled=True)
     own = lax.all_to_all(normed.reshape(across, each, tile_cols, channels), COL, 0, 0, tiled=True)
@@ -305,9 +317,8 @@
     core = lax.axis_index("core")
     even = jnp.where(core == 0, out[0], theirs)
     odd = jnp.where(core == 0, theirs, out[0])
-    update = jnp.stack([even, odd], axis=1).reshape(across, each, tile_cols, channels)
-    update = lax.all_to_all(update, COL, 0, 0, tiled=True)
-    return update.reshape(tile_rows, tile_cols, channels)
+    update = jnp.stack([even, odd], axis=1).reshape(tile_rows, tile_cols, channels)
+    return lax.all_to_all(update, COL, 0, 0, tiled=True)
 
 
 def solution(mesh):

time: 126 us -> 121 us (0.960)
  local copies, waits for them, and re-layouts: 4.01 us -> 0.88 us
  Pallas kernels: 20.7 us -> 18.9 us
    unnamed x25 -> x1, local copies, waits for them, and re-layouts: 2.92 us -> 0.81 us
    pallas_call x1, Pallas kernels: 15.9 us -> 14.1 us  [run_attend(): pl.pallas_call(functools.partial(attend, heads=heads, scale=head ** (-0.5...]
where the time goes in v4:
time: 121 us; the launch traced here: 120 us
  blocking collectives  54.8 us (45%)
  waiting for transfers between devices  33.3 us (28%)
  Pallas kernels  18.9 us (16%)
  starting transfers between devices  11.2 us (9%)
    ppermute x9, waiting for transfers between devices, shifted(): return lax.ppermute(value, axis, [(k, (k + by) % n) for k in range(n)])  32.7 us
    all_to_all x1, blocking collectives, per_device_inner(): return lax.all_to_all(update, COL, 0, 0, tiled=True)  29.6 us
    all_to_all x1, blocking collectives, per_device_inner(): mine = lax.all_to_all(bias, COL, 0, 0, tiled=True)  25.2 us
    pallas_call x1, Pallas kernels, run_attend(): pl.pallas_call(functools.partial(attend, heads=heads, scale=head ** (-0.5...  14.1 us
    ppermute x9, starting transfers between devices, shifted(): return lax.ppermute(value, axis, [(k, (k + by) % n) for k in range(n)])  7.62 us
    pallas_call x1, Pallas kernels, run_prepare(): pl.pallas_call(functools.partial(prepare, step=step), out_shape=(jax.Shap...  4.86 us
    all_to_all x1, starting transfers between devices, per_device_inner(): lax.all_to_all(normed.reshape(across, each, tile_cols, channels), COL, 0,...  3.58 us
  transfers between devices with their start and end apart: 10, of which 7 were waited for; matrix products, arithmetic and copies ran while one was open for 0% of the time, Pallas kernels for 0%

profile of v4, /device:TPU:2, one launch (start us, length us, event | category | flops | bytes accessed | tf_op | source)
XLA Modules:
  0.0 119.9 jit_solution(17540317898044407591)
XLA Ops:
  0.0 4.9 %prepare.1 = (bf16[48,48,128]{2,1,0:T(8,128)(2,1)}, bf16[16,24,384]{2,1,0:T(8,128)(2,1)}) custom-call(bf16[48,48,128]{2,1,0:T(8,128)(2,1)} %pair_hbm.1, f32[1,128]{1,0:T(1,128)} %bitcast.18, bf16[4,128]{1,0:T(4,128)(2,1)} %bitcast.17), custom_call_target="tpu_custom_call" | custom-call | tf_op jit(solution)/shard_map/prepare/pallas_call | solution.py:222
  4.9 25.2 %all_to_all.15.refs_0_ = bf16[16,24,384]{2,1,0:T(8,128)(2,1)S(1)} all-to-all(bf16[16,24,384]{2,1,0:T(8,128)(2,1)} %get-tuple-element.8), channel_id=1, replica_groups=mesh['z_lo'=2,'x'=4,'core'=2,'y'=4,'z_hi'=4] {'y','z_hi'}, dimensions={0} | all-to-all | bytes 589824 | tf_op jit(solution)/shard_map/all_to_all | solution.py:303
  30.0 3.6 %all-to-all-start = ((bf16[16,3,48,128]{3,2,1,0:T(8,128)(2,1)}), bf16[16,3,48,128]{3,2,1,0:T(8,128)(2,1)S(1)}, u32[]{:S(2)}, u32[]{:S(2)}) async-start(bf16[16,3,48,128]{3,2,1,0:T(8,128)(2,1)} %bitcast.2), calls=%async_computation | async-start | bytes 1179648 | tf_op jit(solution)/shard_map/all_to_all | solution.py:304
  33.6 1.1 collective-permute-start.3
  34.7 1.5 %collective-permute-start.1 = (bf16[16,24,384]{2,1,0:T(8,128)(2,1)S(1)}, bf16[16,24,384]{2,1,0:T(8,128)(2,1)S(1)}, u32[]{:S(2)}, u32[]{:S(2)}) collective-permute-start(bf16[16,24,384]{2,1,0:T(8,128)(2,1)S(1)} %all_to_all.15.refs_0_), channel_id=1, source_target_pairs={{0,32},{32,64},{64,96},{96,0},{1,33},{33,65},{65,97},{97,1},{2,34}... | collective-permute-start | bytes 884744 | tf_op jit(solution)/shard_map/ppermute | solution.py:293
  36.2 17.0 %collective-permute-done.3.refs_3_ = bf16[16,24,384]{2,1,0:T(8,128)(2,1)S(1)} collective-permute-done((bf16[16,24,384]{2,1,0:T(8,128)(2,1)S(1)}, bf16[16,24,384]{2,1,0:T(8,128)(2,1)S(1)}, u32[]{:S(2)}, u32[]{:S(2)}) %collective-permute-start.3) | collective-permute-done | bytes 294944 | tf_op jit(solution)/shard_map/ppermute | solution.py:293
  53.2 0.6 collective-permute-start.6
  53.8 0.6 all-to-all-done.own_hbm
  54.4 0.0 collective-permute-start
  54.4 2.2 %collective-permute-start.2 = (bf16[16,24,384]{2,1,0:T(8,128)(2,1)S(1)}, bf16[16,24,384]{2,1,0:T(8,128)(2,1)S(1)}, u32[]{:S(2)}, u32[]{:S(2)}) collective-permute-start(bf16[16,24,384]{2,1,0:T(8,128)(2,1)S(1)} %all_to_all.15.refs_0_), channel_id=1, source_target_pairs={{0,96},{32,0},{64,32},{96,64},{1,97},{33,1},{65,33},{97,65},{2,98}... | collective-permute-start | bytes 884744 | tf_op jit(solution)/shard_map/ppermute | solution.py:293
  56.6 0.0 collective-permute-start.5
  56.6 0.0 collective-permute-done.1.refs_1_
  56.6 1.3 %collective-permute-start.4 = (bf16[16,24,384]{2,1,0:T(8,128)(2,1)S(1)}, bf16[16,24,384]{2,1,0:T(8,128)(2,1)S(1)}, u32[]{:S(2)}, u32[]{:S(2)}) collective-permute-start(bf16[16,24,384]{2,1,0:T(8,128)(2,1)S(1)} %collective-permute-done.1.refs_1_), channel_id=1, source_target_pairs={{0,32},{32,64},{64,96},{96,0},{1,33},{33,65},{65,97},{97,1},{2,34}... | collective-permute-start | bytes 884744 | tf_op jit(solution)/shard_map/ppermute | solution.py:293
  57.9 5.2 %collective-permute-done.6.refs_6_ = bf16[16,24,384]{2,1,0:T(8,128)(2,1)S(1)} collective-permute-done((bf16[16,24,384]{2,1,0:T(8,128)(2,1)S(1)}, bf16[16,24,384]{2,1,0:T(8,128)(2,1)S(1)}, u32[]{:S(2)}, u32[]{:S(2)}) %collective-permute-start.6) | collective-permute-done | bytes 294944 | tf_op jit(solution)/shard_map/ppermute | solution.py:293
  63.1 0.8 collective-permute-start.7
  64.6 4.8 %collective-permute-done.2.refs_0_.refs_2_ = bf16[16,24,384]{2,1,0:T(8,128)(2,1)S(1)} collective-permute-done((bf16[16,24,384]{2,1,0:T(8,128)(2,1)S(1)}, bf16[16,24,384]{2,1,0:T(8,128)(2,1)S(1)}, u32[]{:S(2)}, u32[]{:S(2)}) %collective-permute-start.2) | collective-permute-done | bytes 294944 | tf_op jit(solution)/shard_map/ppermute | solution.py:293
  69.4 0.0 collective-permute-done.5.refs_1_.refs_5_
  69.4 2.6 %collective-permute-done.4.refs_2_.refs_4_ = bf16[16,24,384]{2,1,0:T(8,128)(2,1)S(1)} collective-permute-done((bf16[16,24,384]{2,1,0:T(8,128)(2,1)S(1)}, bf16[16,24,384]{2,1,0:T(8,128)(2,1)S(1)}, u32[]{:S(2)}, u32[]{:S(2)}) %collective-permute-start.4) | collective-permute-done | bytes 294944 | tf_op jit(solution)/shard_map/ppermute | solution.py:293
  72.0 1.5 %collective-permute-done.7.refs_3_.refs_7_ = bf16[16,24,384]{2,1,0:T(8,128)(2,1)S(1)} collective-permute-done((bf16[16,24,384]{2,1,0:T(8,128)(2,1)S(1)}, bf16[16,24,384]{2,1,0:T(8,128)(2,1)S(1)}, u32[]{:S(2)}, u32[]{:S(2)}) %collective-permute-start.7) | collective-permute-done | bytes 294944 | tf_op jit(solution)/shard_map/ppermute | solution.py:293
  73.5 0.0 collective-permute-done.other_hbm
  73.5 14.1 %attend.1 = bf16[2,8,3,48,128]{4,3,2,1,0:T(8,128)(2,1)S(1)} custom-call(s32[1]{0:T(128)S(6)} %copy.12.length_ref, bf16[16,3,48,128]{3,2,1,0:T(8,128)(2,1)S(1)} %all-to-all-done.own_hbm, bf16[16,3,48,128]{3,2,1,0:T(8,128)(2,1)S(1)} %collective-permute-done.other_hbm, bf16[16,24,384]{2,1,0:T(8,128)(2,1)S(1)} %all_to_all.15.refs_0_, ...), custom_call_target="tpu_custom_call" | custom-call | flops 2500000000 | bytes 4000000 | tf_op jit(solution)/shard_map/attend/pallas_call | solution.py:265
  87.6 0.1 collective-permute-start.8
  87.7 1.6 %collective-permute-done.8 = bf16[8,3,48,128]{3,2,1,0:T(8,128)(2,1)S(1)} collective-permute-done((bf16[8,3,48,128]{3,2,1,0:T(8,128)(2,1)S(1)}, bf16[8,3,48,128]{3,2,1,0:T(8,128)(2,1)S(1)}, u32[]{:S(2)}, u32[]{:S(2)}) %collective-permute-start.8) | collective-permute-done | bytes 294944 | tf_op jit(solution)/shard_map/ppermute | solution.py:293
  89.3 0.1 pad_maximum_fusion
  89.4 29.6 %all_to_all.16 = bf16[48,48,128]{2,1,0:T(8,128)(2,1)S(1)} all-to-all(bf16[48,48,128]{2,1,0:T(8,128)(2,1)S(1)} %bitcast.16), channel_id=1, replica_groups=mesh['z_lo'=2,'x'=4,'core'=2,'y'=4,'z_hi'=4] {'y','z_hi'}, dimensions={0} | all-to-all | bytes 1179648 | tf_op jit(solution)/shard_map/all_to_all | solution.py:321
  119.1 0.8 copy.13
  (4 shorter events, 0.1 us)
Async XLA Ops:
  30.0 24.3 %all-to-all-start = ((bf16[16,3,48,128]{3,2,1,0:T(8,128)(2,1)}), bf16[16,3,48,128]{3,2,1,0:T(8,128)(2,1)S(1)}, u32[]{:S(2)}, u32[]{:S(2)}) async-start(bf16[16,3,48,128]{3,2,1,0:T(8,128)(2,1)} %bitcast.2), calls=%async_computation | async-start | bytes 1179648 | tf_op jit(solution)/shard_map/all_to_all | solution.py:304
  33.6 19.6 %collective-permute-start.3 = (bf16[16,24,384]{2,1,0:T(8,128)(2,1)S(1)}, bf16[16,24,384]{2,1,0:T(8,128)(2,1)S(1)}, u32[]{:S(2)}, u32[]{:S(2)}) collective-permute-start(bf16[16,24,384]{2,1,0:T(8,128)(2,1)S(1)} %all_to_all.15.refs_0_), channel_id=1, source_target_pairs={{0,128},{128,0},{1,129},{129,1},{2,130},{130,2},{3,131},{131,3},{4... | collective-permute-start | bytes 884744 | tf_op jit(solution)/shard_map/ppermute | solution.py:293
  34.7 21.9 %collective-permute-start.1 = (bf16[16,24,384]{2,1,0:T(8,128)(2,1)S(1)}, bf16[16,24,384]{2,1,0:T(8,128)(2,1)S(1)}, u32[]{:S(2)}, u32[]{:S(2)}) collective-permute-start(bf16[16,24,384]{2,1,0:T(8,128)(2,1)S(1)} %all_to_all.15.refs_0_), channel_id=1, source_target_pairs={{0,32},{32,64},{64,96},{96,0},{1,33},{33,65},{65,97},{97,1},{2,34}... | collective-permute-start | bytes 884744 | tf_op jit(solution)/shard_map/ppermute | solution.py:293
  53.2 9.9 %collective-permute-start.6 = (bf16[16,24,384]{2,1,0:T(8,128)(2,1)S(1)}, bf16[16,24,384]{2,1,0:T(8,128)(2,1)S(1)}, u32[]{:S(2)}, u32[]{:S(2)}) collective-permute-start(bf16[16,24,384]{2,1,0:T(8,128)(2,1)S(1)} %collective-permute-done.3.refs_3_), channel_id=1, source_target_pairs={{0,96},{32,0},{64,32},{96,64},{1,97},{33,1},{65,33},{97,65},{2,98}... | collective-permute-start | bytes 884744 | tf_op jit(solution)/shard_map/ppermute | solution.py:293
  54.4 19.2 %collective-permute-start = (bf16[16,3,48,128]{3,2,1,0:T(8,128)(2,1)S(1)}, bf16[16,3,48,128]{3,2,1,0:T(8,128)(2,1)S(1)}, u32[]{:S(2)}, u32[]{:S(2)}) collective-permute-start(bf16[16,3,48,128]{3,2,1,0:T(8,128)(2,1)S(1)} %all-to-all-done.own_hbm), channel_id=1, source_target_pairs={{0,16},{16,0},{1,17},{17,1},{2,18},{18,2},{3,19},{19,3},{4,20},{20... | collective-permute-start | bytes 1769480 | tf_op jit(solution)/shard_map/ppermute | solution.py:293
  54.4 15.1 %collective-permute-start.2 = (bf16[16,24,384]{2,1,0:T(8,128)(2,1)S(1)}, bf16[16,24,384]{2,1,0:T(8,128)(2,1)S(1)}, u32[]{:S(2)}, u32[]{:S(2)}) collective-permute-start(bf16[16,24,384]{2,1,0:T(8,128)(2,1)S(1)} %all_to_all.15.refs_0_), channel_id=1, source_target_pairs={{0,96},{32,0},{64,32},{96,64},{1,97},{33,1},{65,33},{97,65},{2,98}... | collective-permute-start | bytes 884744 | tf_op jit(solution)/shard_map/ppermute | solution.py:293
  56.6 12.9 %collective-permute-start.5 = (bf16[16,24,384]{2,1,0:T(8,128)(2,1)S(1)}, bf16[16,24,384]{2,1,0:T(8,128)(2,1)S(1)}, u32[]{:S(2)}, u32[]{:S(2)}) collective-permute-start(bf16[16,24,384]{2,1,0:T(8,128)(2,1)S(1)} %collective-permute-done.3.refs_3_), channel_id=1, source_target_pairs={{0,32},{32,64},{64,96},{96,0},{1,33},{33,65},{65,97},{97,1},{2,34}... | collective-permute-start | bytes 884744 | tf_op jit(solution)/shard_map/ppermute | solution.py:293
  56.6 15.5 %collective-permute-start.4 = (bf16[16,24,384]{2,1,0:T(8,128)(2,1)S(1)}, bf16[16,24,384]{2,1,0:T(8,128)(2,1)S(1)}, u32[]{:S(2)}, u32[]{:S(2)}) collective-permute-start(bf16[16,24,384]{2,1,0:T(8,128)(2,1)S(1)} %collective-permute-done.1.refs_1_), channel_id=1, source_target_pairs={{0,32},{32,64},{64,96},{96,0},{1,33},{33,65},{65,97},{97,1},{2,34}... | collective-permute-start | bytes 884744 | tf_op jit(solution)/shard_map/ppermute | solution.py:293
  63.1 10.4 %collective-permute-start.7 = (bf16[16,24,384]{2,1,0:T(8,128)(2,1)S(1)}, bf16[16,24,384]{2,1,0:T(8,128)(2,1)S(1)}, u32[]{:S(2)}, u32[]{:S(2)}) collective-permute-start(bf16[16,24,384]{2,1,0:T(8,128)(2,1)S(1)} %collective-permute-done.6.refs_6_), channel_id=1, source_target_pairs={{0,96},{32,0},{64,32},{96,64},{1,97},{33,1},{65,33},{97,65},{2,98}... | collective-permute-start | bytes 884744 | tf_op jit(solution)/shard_map/ppermute | solution.py:293
  87.6 1.7 %collective-permute-start.8 = (bf16[8,3,48,128]{3,2,1,0:T(8,128)(2,1)S(1)}, bf16[8,3,48,128]{3,2,1,0:T(8,128)(2,1)S(1)}, u32[]{:S(2)}, u32[]{:S(2)}) collective-permute-start(bf16[8,3,48,128]{3,2,1,0:T(8,128)(2,1)S(1)} %slice_bitcast_fusion), channel_id=1, source_target_pairs={{0,16},{16,0},{1,17},{17,1},{2,18},{18,2},{3,19},{19,3},{4,20},{20... | collective-permute-start | bytes 884744 | tf_op jit(solution)/shard_map/ppermute | solution.py:293

commit v5 on v4

--- a/solution.py
+++ b/solution.py
@@ -14,8 +14,8 @@
     return lax.dot_general(a, b, (((da,), (db,)), ((), ())), preferred_element_type=f32)
 
 
-def prepare(pair_hbm, gain_ref, w_ref, normed_hbm, bias_hbm, *refs, step):
-    pair_ref, sems, normed_ref, normed_sems, bias_ref, bias_sems, wide_ref = refs
+def prepare(pair_hbm, gain_hbm, w_hbm, normed_hbm, bias_out, *refs, step):
+    pair_ref, sems, normed_ref, normed_sems, gain_ref, w_ref, small_sems, wide_ref = refs
     rows, cols, channels = pair_ref.shape
     heads = w_ref.shape[0]
     half = cols // 2
@@ -24,8 +24,14 @@
         pltpu.make_async_copy(pair_hbm.at[pl.ds(g * step, step)], pair_ref.at[pl.ds(g * step, step)], sems.at[g])
         for g in range(rows // step)
     ]
-    for fetch in fetches:
+    small = [
+        pltpu.make_async_copy(w_hbm, w_ref, small_sems.at[0]),
+        pltpu.make_async_copy(gain_hbm, gain_ref, small_sems.at[1]),
+    ]
+    for fetch in fetches[:1] + small + fetches[1:]:
         fetch.start()
+    for fetch in small:
+        fetch.wait()
     gain = gain_ref[...]
     slots = 2 * heads
     mine = lax.axis_index("z_lo") * lax.axis_size("x") + lax.axis_index("x")
@@ -56,10 +62,9 @@
             one = wide[t * cols : (t + 1) * cols]
             both = jnp.where(first, one[:half], one[half:])
             acc = jnp.where(lane_j == start + t, both, acc)
-    bias_ref[...] = acc.astype(bf16)
-    for c in range(bias_hbm.shape[0]):
-        stores.append(pltpu.make_async_copy(bias_ref, bias_hbm.at[c], bias_sems.at[c]))
-        stores[-1].start()
+    bias = acc.astype(bf16)
+    for c in range(bias_out.shape[0]):
+        bias_out[c] = bias
     for store in stores:
         store.wait()
 
@@ -116,101 +121,101 @@
                     table[h, pl.ds(start, half), n * 128 : (n + 1) * 128] = jnp.where(valid, value, -1e30)
         return carry
 
-    lax.fori_loop(0, blocks, build, 0)
+    sizes = [keys * n // 6 for n in (4, 5, 6)]
+    filled = jnp.int32(blocks)
+    for used in reversed(sizes[:-1]):
+        filled = jnp.where(length <= used, -(-used // width), filled)
+    lax.fori_loop(0, filled, build, 0)
     for copy in later:
         copy.wait()
-    chunk = keys // 2
-    steps = keys // chunk
     wq, wk, wo = weights[0], weights[1], weights[4]
     wv = weights[2].T
     wg = weights[3].T
     lane = lax.broadcasted_iota(jnp.int32, (width, channels), 1)
     of_head = [(lane >= h * head) & (lane < (h + 1) * head) for h in range(heads)]
 
-    def cells(n, chosen):
-        side, t = n // each, lax.rem(n, each)
-        return jnp.concatenate([both[side, c, t] for c in chosen], axis=0)
-
-    def project_keys(n, to):
-        keys_of[to][...] = contract(cells(n, range(blocks)), wk, 1, 0).astype(bf16)
-
-    def project_values(n, to):
-        value = contract(wv, cells(n, range(blocks)), 1, 1).astype(bf16)
-        for h in range(heads):
-            values_of[to][h, :head] = value[h * head : (h + 1) * head]
-
-    def project_queries(n, to):
-        asked = cells(n, [2 * q + core for q in range(slots)])
-        query = (contract(asked, wq, 1, 0) * scale).astype(bf16)
-        for h in range(heads):
-            for p in range(slots):
-                q = (p - h) % slots
-                block = query[q * width : (q + 1) * width]
-                queries_of[to][h, p * width : (p + 1) * width] = jnp.where(of_head[h], block, jnp.zeros_like(block))
-
-    def project_gates(n, to):
-        asked = cells(n, [2 * q + core for q in range(slots)])
-        gates_of[to][...] = jax.nn.sigmoid(contract(wg, asked, 1, 1)).astype(bf16).astype(f32)
-
-    def score(at, h, k, top):
-        part = pl.ds(k * chunk, chunk)
-        scores = contract(keys_of[at][part], queries_of[at][h], 1, 1) + table[h, part]
-        scores_of[h % 2][part] = scores
-        best = jnp.max(scores.reshape(chunk // 8, 8, queries), 0)
-        return best if top is None else jnp.maximum(top, best)
-
-    def blend(at, h, k, highest, sofar):
-        exponent = jnp.exp(scores_of[h % 2][pl.ds(k * chunk, chunk)] - highest).astype(bf16)
-        more = contract(values_of[at][h, :, k * chunk : (k + 1) * chunk], exponent, 1, 0)
-        return more if sofar is None else sofar + more
-
-    def one_row(n, at, top):
-        following = jnp.minimum(n + 1, 2 * each - 1)
-        for h in range(heads):
-            highest = jnp.max(top, 0, keepdims=True)
-            top, total = None, None
-            for k in range(steps):
-                if h + 1 < heads:
-                    top = score(at, h + 1, k, top)
-                else:
-                    top = score(1 - at, 0, k, top)
-                total = blend(at, h, k, highest, total)
-                if h == 0 and k == 0:
+    def all_rows(used):
+        def cells(n, chosen):
+            side, t = n // each, lax.rem(n, each)
+            return jnp.concatenate([both[side, c, t] for c in chosen], axis=0)
+
+        def project_keys(n, to):
+            keys_of[to][:used] = contract(cells(n, range(-(-used // width)))[:used], wk, 1, 0).astype(bf16)
+
+        def project_values(n, to):
+            value = contract(wv, cells(n, range(-(-used // width)))[:used], 1, 1).astype(bf16)
+            for h in range(heads):
+                values_of[to][h, :head, :used] = value[h * head : (h + 1) * head]
+
+        def project_queries(n, to):
+            asked = cells(n, [2 * q + core for q in range(slots)])
+            query = (contract(asked, wq, 1, 0) * scale).astype(bf16)
+            for h in range(heads):
+                for p in range(slots):
+                    q = (p - h) % slots
+                    block = query[q * width : (q + 1) * width]
+                    queries_of[to][h, p * width : (p + 1) * width] = jnp.where(of_head[h], block, jnp.zeros_like(block))
+
+        def project_gates(n, to):
+            asked = cells(n, [2 * q + core for q in range(slots)])
+            gates_of[to][...] = jax.nn.sigmoid(contract(wg, asked, 1, 1)).astype(bf16).astype(f32)
+
+        def score(at, h):
+            scores = contract(keys_of[at][:used], queries_of[at][h], 1, 1) + table[h, :used]
+            scores_of[h % 2][:used] = scores
+            return jnp.max(scores.reshape(used // 8, 8, queries), 0)
+
+        def blend(at, h, highest):
+            exponent = jnp.exp(scores_of[h % 2][:used] - highest).astype(bf16)
+            return contract(values_of[at][h, :, :used], exponent, 1, 0)
+
+        def one_row(n, at, top):
+            following = jnp.minimum(n + 1, 2 * each - 1)
+            for h in range(heads):
+                highest = jnp.max(top, 0, keepdims=True)
+                top = score(at, h + 1) if h + 1 < heads else score(1 - at, 0)
+                total = blend(at, h, highest)
+                if h == 0:
                     project_keys(following, 1 - at)
-                if h == 0 and k == 1:
                     project_queries(following, 1 - at)
-                if h == 1 and k == 0:
+                if h == 1:
                     project_values(following, 1 - at)
-                if h == 2 and k == 0:
+                if h == 2:
                     project_gates(following, 1 - at)
-            blended = total[:head] / total[head : head + 1]
-            if h > 0:
-                blended = jnp.concatenate([blended[:, h * width :], blended[:, : h * width]], axis=1)
-            part = slice(h * head, (h + 1) * head)
-            gated_of[at][part] = (gates_of[at][part] * blended).astype(bf16)
-        update = contract(gated_of[at][...], wo, 0, 0)
-        side, t = n // each, lax.rem(n, each)
-        row_ok = jnp.where(side == 0, own_base, other_base) + t < length
-        row = lax.broadcasted_iota(jnp.int32, (width, channels), 0)
-        for q in range(slots):
-            ok = (row + (2 * q + core) * width < length) & row_ok
-            piece = update[q * width : (q + 1) * width]
-            out_ref[side, q, t] = jnp.where(ok, piece, 0.0).astype(bf16)
-        return top
-
-    for first in (project_keys, project_queries, project_values, project_gates):
-        first(0, 0)
-    top = None
-    for k in range(steps):
-        top = score(0, 0, k, top)
-    lax.fori_loop(0, each, lambda n, top: one_row(2 * n + 1, 1, one_row(2 * n, 0, top)), top)
+                blended = total[:head] / total[head : head + 1]
+                if h > 0:
+                    blended = jnp.concatenate([blended[:, h * width :], blended[:, : h * width]], axis=1)
+                part = slice(h * head, (h + 1) * head)
+                gated_of[at][part] = (gates_of[at][part] * blended).astype(bf16)
+            update = contract(gated_of[at][...], wo, 0, 0)
+            side, t = n // each, lax.rem(n, each)
+            row_ok = jnp.where(side == 0, own_base, other_base) + t < length
+            row = lax.broadcasted_iota(jnp.int32, (width, channels), 0)
+            for q in range(slots):
+                ok = (row + (2 * q + core) * width < length) & row_ok
+                piece = update[q * width : (q + 1) * width]
+                out_ref[side, q, t] = jnp.where(ok, piece, 0.0).astype(bf16)
+            return top
+
+        for first in (project_keys, project_queries, project_values, project_gates):
+            first(0, 0)
+        lax.fori_loop(0, each, lambda n, top: one_row(2 * n + 1, 1, one_row(2 * n, 0, top)), score(0, 0))
+
+    for n, used in enumerate(sizes):
+        fits = length <= used
+        if n > 0:
+            fits = fits & (length > sizes[n - 1])
+        pl.when(fits)(functools.partial(all_rows, used))
 
 
 ROW, COL = ("z_lo", "x", "core"), ("y", "z_hi")
-ALL_VMEM = 67043328
 VMEM = pl.BlockSpec(memory_space=pltpu.VMEM)
 HBM = pl.BlockSpec(memory_space=pltpu.HBM)
 SMEM = pl.BlockSpec(memory_space=pltpu.SMEM)
+
+
+def in_hbm(value):
+    return pltpu.with_memory_space_constraint(value, pltpu.HBM)
 
 
 def run_prepare(pair, ln_gain, w_bias, across):
@@ -225,20 +230,21 @@
             jax.ShapeDtypeStruct(pair.shape, bf16),
             jax.ShapeDtypeStruct((across, half, lanes), bf16),
         ),
-        in_specs=[HBM, pl.BlockSpec(), pl.BlockSpec()],
-        out_specs=(HBM, HBM),
+        in_specs=[HBM] * 3,
+        out_specs=(HBM, VMEM),
         scratch_shapes=[
             pltpu.VMEM(pair.shape, bf16),
             pltpu.SemaphoreType.DMA((tile_rows // step,)),
             pltpu.VMEM(pair.shape, bf16),
             pltpu.SemaphoreType.DMA((tile_rows // step,)),
-            pltpu.VMEM((half, lanes), bf16),
-            pltpu.SemaphoreType.DMA((across,)),
+            pltpu.VMEM((1, channels), f32),
+            pltpu.VMEM((heads, channels), bf16),
+            pltpu.SemaphoreType.DMA((2,)),
             pltpu.VMEM((channels, lanes), bf16),
         ],
-        compiler_params=pltpu.CompilerParams(vmem_limit_bytes=ALL_VMEM),
+        compiler_params=pltpu.CompilerParams(vmem_limit_bytes=16 << 20),
         name="prepare",
-    )(pair, ln_gain.reshape(1, channels), w_bias.T)
+    )(*[in_hbm(v) for v in (pair, ln_gain.reshape(1, channels), w_bias.T)])
 
 
 def order_of_slots(z, along):
@@ -298,7 +304,7 @@
     heads = w_bias.shape[1]
     across = lax.axis_size(COL)
     each = tile_rows // across
-    weights = [pltpu.with_memory_space_constraint(w, pltpu.HBM) for w in (w_query, w_key, w_value, w_gate, w_out)]
+    weights = [in_hbm(w) for w in (w_query, w_key, w_value, w_gate, w_out)]
     normed, bias = run_prepare(pair, ln_gain, w_bias, across)
     mine = lax.all_to_all(bias, COL, 0, 0, tiled=True)
     own = lax.all_to_all(normed.reshape(across, each, tile_cols, channels), COL, 0, 0, tiled=True)

time: 121 us -> 120 us (level)
  Pallas kernels: 18.9 us -> 17.5 us
where the time goes in v5:
time: 120 us; the launch traced here: 118 us
  blocking collectives  54.5 us (45%)
  waiting for transfers between devices  33.4 us (28%)
  Pallas kernels  17.5 us (15%)
  starting transfers between devices  11.1 us (9%)
    ppermute x9, waiting for transfers between devices, shifted(): return lax.ppermute(value, axis, [(k, (k + by) % n) for k in range(n)])  32.8 us
    all_to_all x1, blocking collectives, per_device_inner(): return lax.all_to_all(update, COL, 0, 0, tiled=True)  29.6 us
    all_to_all x1, blocking collectives, per_device_inner(): mine = lax.all_to_all(bias, COL, 0, 0, tiled=True)  25 us
    pallas_call x1, Pallas kernels, run_attend(): pl.pallas_call(functools.partial(attend, heads=heads, scale=head ** (-0.5...  13.5 us
    ppermute x9, starting transfers between devices, shifted(): return lax.ppermute(value, axis, [(k, (k + by) % n) for k in range(n)])  7.52 us
    pallas_call x1, Pallas kernels, run_prepare(): pl.pallas_call(functools.partial(prepare, step=step), out_shape=(jax.Shap...  4.08 us
    all_to_all x1, starting transfers between devices, per_device_inner(): lax.all_to_all(normed.reshape(across, each, tile_cols, channels), COL, 0,...  3.58 us
  transfers between devices with their start and end apart: 10, of which 7 were waited for; matrix products, arithmetic and copies ran while one was open for 0% of the time, Pallas kernels for 0%

profile of v5, /device:TPU:2, one launch (start us, length us, event | category | flops | bytes accessed | tf_op | source)
XLA Modules:
  0.0 118.3 jit_solution(13036743782602746512)
XLA Ops:
  0.0 4.1 %prepare.1 = (bf16[48,48,128]{2,1,0:T(8,128)(2,1)}, bf16[16,24,384]{2,1,0:T(8,128)(2,1)S(1)}) custom-call(bf16[48,48,128]{2,1,0:T(8,128)(2,1)} %pair_hbm.1, f32[1,128]{1,0:T(1,128)} %bitcast.18, bf16[4,128]{1,0:T(4,128)(2,1)} %bitcast.17), custom_call_target="tpu_custom_call" | custom-call | tf_op jit(solution)/shard_map/prepare/pallas_call | solution.py:227
  4.1 25.0 %all_to_all.15.refs_0_ = bf16[16,24,384]{2,1,0:T(8,128)(2,1)S(1)} all-to-all(bf16[16,24,384]{2,1,0:T(8,128)(2,1)S(1)} %get-tuple-element.8), channel_id=1, replica_groups=mesh['z_lo'=2,'x'=4,'core'=2,'y'=4,'z_hi'=4] {'y','z_hi'}, dimensions={0} | all-to-all | bytes 589824 | tf_op jit(solution)/shard_map/all_to_all | solution.py:309
  29.0 3.6 %all-to-all-start = ((bf16[16,3,48,128]{3,2,1,0:T(8,128)(2,1)}), bf16[16,3,48,128]{3,2,1,0:T(8,128)(2,1)S(1)}, u32[]{:S(2)}, u32[]{:S(2)}) async-start(bf16[16,3,48,128]{3,2,1,0:T(8,128)(2,1)} %bitcast.2), calls=%async_computation | async-start | bytes 1179648 | tf_op jit(solution)/shard_map/all_to_all | solution.py:310
  32.6 1.1 collective-permute-start.3
  33.7 1.5 %collective-permute-start.1 = (bf16[16,24,384]{2,1,0:T(8,128)(2,1)S(1)}, bf16[16,24,384]{2,1,0:T(8,128)(2,1)S(1)}, u32[]{:S(2)}, u32[]{:S(2)}) collective-permute-start(bf16[16,24,384]{2,1,0:T(8,128)(2,1)S(1)} %all_to_all.15.refs_0_), channel_id=1, source_target_pairs={{0,32},{32,64},{64,96},{96,0},{1,33},{33,65},{65,97},{97,1},{2,34}... | collective-permute-start | bytes 884744 | tf_op jit(solution)/shard_map/ppermute | solution.py:299
  35.2 17.0 %collective-permute-done.3.refs_3_ = bf16[16,24,384]{2,1,0:T(8,128)(2,1)S(1)} collective-permute-done((bf16[16,24,384]{2,1,0:T(8,128)(2,1)S(1)}, bf16[16,24,384]{2,1,0:T(8,128)(2,1)S(1)}, u32[]{:S(2)}, u32[]{:S(2)}) %collective-permute-start.3) | collective-permute-done | bytes 294944 | tf_op jit(solution)/shard_map/ppermute | solution.py:299
  52.3 0.5 collective-permute-start.6
  52.8 0.6 all-to-all-done.own_hbm
  53.4 0.0 collective-permute-start
  53.4 2.1 %collective-permute-start.2 = (bf16[16,24,384]{2,1,0:T(8,128)(2,1)S(1)}, bf16[16,24,384]{2,1,0:T(8,128)(2,1)S(1)}, u32[]{:S(2)}, u32[]{:S(2)}) collective-permute-start(bf16[16,24,384]{2,1,0:T(8,128)(2,1)S(1)} %all_to_all.15.refs_0_), channel_id=1, source_target_pairs={{0,96},{32,0},{64,32},{96,64},{1,97},{33,1},{65,33},{97,65},{2,98}... | collective-permute-start | bytes 884744 | tf_op jit(solution)/shard_map/ppermute | solution.py:299
  55.6 0.0 collective-permute-start.5
  55.6 0.0 collective-permute-done.1.refs_1_
  55.6 1.4 %collective-permute-start.4 = (bf16[16,24,384]{2,1,0:T(8,128)(2,1)S(1)}, bf16[16,24,384]{2,1,0:T(8,128)(2,1)S(1)}, u32[]{:S(2)}, u32[]{:S(2)}) collective-permute-start(bf16[16,24,384]{2,1,0:T(8,128)(2,1)S(1)} %collective-permute-done.1.refs_1_), channel_id=1, source_target_pairs={{0,32},{32,64},{64,96},{96,0},{1,33},{33,65},{65,97},{97,1},{2,34}... | collective-permute-start | bytes 884744 | tf_op jit(solution)/shard_map/ppermute | solution.py:299
  56.9 5.2 %collective-permute-done.6.refs_6_ = bf16[16,24,384]{2,1,0:T(8,128)(2,1)S(1)} collective-permute-done((bf16[16,24,384]{2,1,0:T(8,128)(2,1)S(1)}, bf16[16,24,384]{2,1,0:T(8,128)(2,1)S(1)}, u32[]{:S(2)}, u32[]{:S(2)}) %collective-permute-start.6) | collective-permute-done | bytes 294944 | tf_op jit(solution)/shard_map/ppermute | solution.py:299
  62.1 0.8 collective-permute-start.7
  63.6 4.9 %collective-permute-done.2.refs_0_.refs_2_ = bf16[16,24,384]{2,1,0:T(8,128)(2,1)S(1)} collective-permute-done((bf16[16,24,384]{2,1,0:T(8,128)(2,1)S(1)}, bf16[16,24,384]{2,1,0:T(8,128)(2,1)S(1)}, u32[]{:S(2)}, u32[]{:S(2)}) %collective-permute-start.2) | collective-permute-done | bytes 294944 | tf_op jit(solution)/shard_map/ppermute | solution.py:299
  68.5 0.0 collective-permute-done.5.refs_1_.refs_5_
  68.5 2.5 %collective-permute-done.4.refs_2_.refs_4_ = bf16[16,24,384]{2,1,0:T(8,128)(2,1)S(1)} collective-permute-done((bf16[16,24,384]{2,1,0:T(8,128)(2,1)S(1)}, bf16[16,24,384]{2,1,0:T(8,128)(2,1)S(1)}, u32[]{:S(2)}, u32[]{:S(2)}) %collective-permute-start.4) | collective-permute-done | bytes 294944 | tf_op jit(solution)/shard_map/ppermute | solution.py:299
  71.0 1.5 %collective-permute-done.7.refs_3_.refs_7_ = bf16[16,24,384]{2,1,0:T(8,128)(2,1)S(1)} collective-permute-done((bf16[16,24,384]{2,1,0:T(8,128)(2,1)S(1)}, bf16[16,24,384]{2,1,0:T(8,128)(2,1)S(1)}, u32[]{:S(2)}, u32[]{:S(2)}) %collective-permute-start.7) | collective-permute-done | bytes 294944 | tf_op jit(solution)/shard_map/ppermute | solution.py:299
  72.6 0.0 collective-permute-done.other_hbm
  72.6 13.5 %attend.1 = bf16[2,8,3,48,128]{4,3,2,1,0:T(8,128)(2,1)S(1)} custom-call(s32[1]{0:T(128)S(6)} %copy.12.length_ref, bf16[16,3,48,128]{3,2,1,0:T(8,128)(2,1)S(1)} %all-to-all-done.own_hbm, bf16[16,3,48,128]{3,2,1,0:T(8,128)(2,1)S(1)} %collective-permute-done.other_hbm, bf16[16,24,384]{2,1,0:T(8,128)(2,1)S(1)} %all_to_all.15.refs_0_, ...), custom_call_target="tpu_custom_call" | custom-call | flops 2500000000 | bytes 4000000 | tf_op jit(solution)/shard_map/attend/pallas_call | solution.py:271
  86.1 0.1 collective-permute-start.8
  86.2 1.6 %collective-permute-done.8 = bf16[8,3,48,128]{3,2,1,0:T(8,128)(2,1)S(1)} collective-permute-done((bf16[8,3,48,128]{3,2,1,0:T(8,128)(2,1)S(1)}, bf16[8,3,48,128]{3,2,1,0:T(8,128)(2,1)S(1)}, u32[]{:S(2)}, u32[]{:S(2)}) %collective-permute-start.8) | collective-permute-done | bytes 294944 | tf_op jit(solution)/shard_map/ppermute | solution.py:299
  87.8 0.1 pad_maximum_fusion
  87.9 29.6 %all_to_all.16 = bf16[48,48,128]{2,1,0:T(8,128)(2,1)S(1)} all-to-all(bf16[48,48,128]{2,1,0:T(8,128)(2,1)S(1)} %bitcast.16), channel_id=1, replica_groups=mesh['z_lo'=2,'x'=4,'core'=2,'y'=4,'z_hi'=4] {'y','z_hi'}, dimensions={0} | all-to-all | bytes 1179648 | tf_op jit(solution)/shard_map/all_to_all | solution.py:327
  117.5 0.8 copy.13
  (4 shorter events, 0.1 us)
Async XLA Ops:
  29.0 24.4 %all-to-all-start = ((bf16[16,3,48,128]{3,2,1,0:T(8,128)(2,1)}), bf16[16,3,48,128]{3,2,1,0:T(8,128)(2,1)S(1)}, u32[]{:S(2)}, u32[]{:S(2)}) async-start(bf16[16,3,48,128]{3,2,1,0:T(8,128)(2,1)} %bitcast.2), calls=%async_computation | async-start | bytes 1179648 | tf_op jit(solution)/shard_map/all_to_all | solution.py:310
  32.6 19.6 %collective-permute-start.3 = (bf16[16,24,384]{2,1,0:T(8,128)(2,1)S(1)}, bf16[16,24,384]{2,1,0:T(8,128)(2,1)S(1)}, u32[]{:S(2)}, u32[]{:S(2)}) collective-permute-start(bf16[16,24,384]{2,1,0:T(8,128)(2,1)S(1)} %all_to_all.15.refs_0_), channel_id=1, source_target_pairs={{0,128},{128,0},{1,129},{129,1},{2,130},{130,2},{3,131},{131,3},{4... | collective-permute-start | bytes 884744 | tf_op jit(solution)/shard_map/ppermute | solution.py:299
  33.7 21.8 %collective-permute-start.1 = (bf16[16,24,384]{2,1,0:T(8,128)(2,1)S(1)}, bf16[16,24,384]{2,1,0:T(8,128)(2,1)S(1)}, u32[]{:S(2)}, u32[]{:S(2)}) collective-permute-start(bf16[16,24,384]{2,1,0:T(8,128)(2,1)S(1)} %all_to_all.15.refs_0_), channel_id=1, source_target_pairs={{0,32},{32,64},{64,96},{96,0},{1,33},{33,65},{65,97},{97,1},{2,34}... | collective-permute-start | bytes 884744 | tf_op jit(solution)/shard_map/ppermute | solution.py:299
  52.3 9.9 %collective-permute-start.6 = (bf16[16,24,384]{2,1,0:T(8,128)(2,1)S(1)}, bf16[16,24,384]{2,1,0:T(8,128)(2,1)S(1)}, u32[]{:S(2)}, u32[]{:S(2)}) collective-permute-start(bf16[16,24,384]{2,1,0:T(8,128)(2,1)S(1)} %collective-permute-done.3.refs_3_), channel_id=1, source_target_pairs={{0,96},{32,0},{64,32},{96,64},{1,97},{33,1},{65,33},{97,65},{2,98}... | collective-permute-start | bytes 884744 | tf_op jit(solution)/shard_map/ppermute | solution.py:299
  53.4 19.2 %collective-permute-start = (bf16[16,3,48,128]{3,2,1,0:T(8,128)(2,1)S(1)}, bf16[16,3,48,128]{3,2,1,0:T(8,128)(2,1)S(1)}, u32[]{:S(2)}, u32[]{:S(2)}) collective-permute-start(bf16[16,3,48,128]{3,2,1,0:T(8,128)(2,1)S(1)} %all-to-all-done.own_hbm), channel_id=1, source_target_pairs={{0,16},{16,0},{1,17},{17,1},{2,18},{18,2},{3,19},{19,3},{4,20},{20... | collective-permute-start | bytes 1769480 | tf_op jit(solution)/shard_map/ppermute | solution.py:299
  53.4 15.1 %collective-permute-start.2 = (bf16[16,24,384]{2,1,0:T(8,128)(2,1)S(1)}, bf16[16,24,384]{2,1,0:T(8,128)(2,1)S(1)}, u32[]{:S(2)}, u32[]{:S(2)}) collective-permute-start(bf16[16,24,384]{2,1,0:T(8,128)(2,1)S(1)} %all_to_all.15.refs_0_), channel_id=1, source_target_pairs={{0,96},{32,0},{64,32},{96,64},{1,97},{33,1},{65,33},{97,65},{2,98}... | collective-permute-start | bytes 884744 | tf_op jit(solution)/shard_map/ppermute | solution.py:299
  55.6 12.9 %collective-permute-start.5 = (bf16[16,24,384]{2,1,0:T(8,128)(2,1)S(1)}, bf16[16,24,384]{2,1,0:T(8,128)(2,1)S(1)}, u32[]{:S(2)}, u32[]{:S(2)}) collective-permute-start(bf16[16,24,384]{2,1,0:T(8,128)(2,1)S(1)} %collective-permute-done.3.refs_3_), channel_id=1, source_target_pairs={{0,32},{32,64},{64,96},{96,0},{1,33},{33,65},{65,97},{97,1},{2,34}... | collective-permute-start | bytes 884744 | tf_op jit(solution)/shard_map/ppermute | solution.py:299
  55.6 15.5 %collective-permute-start.4 = (bf16[16,24,384]{2,1,0:T(8,128)(2,1)S(1)}, bf16[16,24,384]{2,1,0:T(8,128)(2,1)S(1)}, u32[]{:S(2)}, u32[]{:S(2)}) collective-permute-start(bf16[16,24,384]{2,1,0:T(8,128)(2,1)S(1)} %collective-permute-done.1.refs_1_), channel_id=1, source_target_pairs={{0,32},{32,64},{64,96},{96,0},{1,33},{33,65},{65,97},{97,1},{2,34}... | collective-permute-start | bytes 884744 | tf_op jit(solution)/shard_map/ppermute | solution.py:299
  62.1 10.4 %collective-permute-start.7 = (bf16[16,24,384]{2,1,0:T(8,128)(2,1)S(1)}, bf16[16,24,384]{2,1,0:T(8,128)(2,1)S(1)}, u32[]{:S(2)}, u32[]{:S(2)}) collective-permute-start(bf16[16,24,384]{2,1,0:T(8,128)(2,1)S(1)} %collective-permute-done.6.refs_6_), channel_id=1, source_target_pairs={{0,96},{32,0},{64,32},{96,64},{1,97},{33,1},{65,33},{97,65},{2,98}... | collective-permute-start | bytes 884744 | tf_op jit(solution)/shard_map/ppermute | solution.py:299
  86.1 1.7 %collective-permute-start.8 = (bf16[8,3,48,128]{3,2,1,0:T(8,128)(2,1)S(1)}, bf16[8,3,48,128]{3,2,1,0:T(8,128)(2,1)S(1)}, u32[]{:S(2)}, u32[]{:S(2)}) collective-permute-start(bf16[8,3,48,128]{3,2,1,0:T(8,128)(2,1)S(1)} %slice_bitcast_fusion), channel_id=1, source_target_pairs={{0,16},{16,0},{1,17},{17,1},{2,18},{18,2},{3,19},{19,3},{4,20},{20... | collective-permute-start | bytes 884744 | tf_op jit(solution)/shard_map/ppermute | solution.py:299

commit v6 on v5

--- a/solution.py
+++ b/solution.py
@@ -14,16 +14,14 @@
     return lax.dot_general(a, b, (((da,), (db,)), ((), ())), preferred_element_type=f32)
 
 
-def prepare(pair_hbm, gain_hbm, w_hbm, normed_hbm, bias_out, *refs, step):
+def prepare(pair_hbm, gain_hbm, w_hbm, normed_hbm, bias_out, *refs, cuts):
     pair_ref, sems, normed_ref, normed_sems, gain_ref, w_ref, small_sems, wide_ref = refs
     rows, cols, channels = pair_ref.shape
     heads = w_ref.shape[0]
     half = cols // 2
     lanes = wide_ref.shape[1]
-    fetches = [
-        pltpu.make_async_copy(pair_hbm.at[pl.ds(g * step, step)], pair_ref.at[pl.ds(g * step, step)], sems.at[g])
-        for g in range(rows // step)
-    ]
+    runs = [pl.ds(start, stop - start) for start, stop in zip(cuts, cuts[1:])]
+    fetches = [pltpu.make_async_copy(pair_hbm.at[r], pair_ref.at[r], sems.at[g]) for g, r in enumerate(runs)]
     small = [
         pltpu.make_async_copy(w_hbm, w_ref, small_sems.at[0]),
         pltpu.make_async_copy(gain_hbm, gain_ref, small_sems.at[1]),
@@ -48,7 +46,7 @@
     stores = []
     for g, fetch in enumerate(fetches):
         fetch.wait()
-        start = g * step
+        start, step = cuts[g], cuts[g + 1] - cuts[g]
         x = pair_ref[pl.ds(start, step)].reshape(step * cols, channels).astype(f32)
         centred = x - jnp.mean(x, -1, keepdims=True)
         spread = jnp.mean(centred * centred, -1, keepdims=True)
@@ -73,31 +71,24 @@
     refs[-1][...] = jnp.zeros_like(refs[-1])
 
 
-def attend(length_ref, own_hbm, other_hbm, *refs, heads, scale, slots):
-    parts_hbm, weights_hbm, refs = refs[:slots], refs[slots : slots + 5], refs[slots + 6 :]
-    out_ref, weights, sems, parts, part_sems, both, both_sems = refs[:7]
-    table = refs[7]
-    keys_of, values_of, queries_of, gates_of, gated_of, scores_of = [refs[n : n + 2] for n in range(8, 20, 2)]
-    _, blocks, each, width, channels = both.shape
-    half = width // 2
-    head = channels // heads
-    keys, queries = blocks * width, slots * width
-    core, x, z = lax.axis_index("core"), lax.axis_index("x"), lax.axis_index("z_lo")
+def key_sizes(keys):
+    return [keys * n // 6 for n in (4, 5, 6)]
+
+
+def build_table(length_ref, *refs, heads, width):
+    slots = len(refs) - 3
+    parts_in, (table, parts, part_sems) = refs[:slots], refs[slots:]
+    _, blocks, half, queries = parts.shape
+    keys = blocks * width
+    x, z = lax.axis_index("x"), lax.axis_index("z_lo")
     along = lax.axis_size("x")
     places = [zz * along + lax.rem(x + by, along) for zz, by in order_of_slots(z, along)]
-    fetches = [pltpu.make_async_copy(p, parts.at[q], part_sems.at[n]) for n, (p, q) in enumerate(zip(parts_hbm, places))]
-    later = [pltpu.make_async_copy(w, weights.at[n], sems.at[n]) for n, w in enumerate(weights_hbm)]
-    later += [pltpu.make_async_copy(r, both.at[n], both_sems.at[n]) for n, r in enumerate((own_hbm, other_hbm))]
-    for copy in fetches + later:
-        copy.start()
+    fetches = [pltpu.make_async_copy(p, parts.at[q], part_sems.at[n]) for n, (p, q) in enumerate(zip(parts_in, places))]
+    for fetch in fetches:
+        fetch.start()
     length = length_ref[0]
-    base = (lax.axis_index("y") * lax.axis_size("z_hi") + lax.axis_index("z_hi")) * each
-    own_base = (2 * (z * along + x) + core) * (each * blocks) + base
-    other_base = (2 * (z * along + x) + 1 - core) * (each * blocks) + base
-    for ref in values_of:
-        ref[:, head:] = jnp.ones_like(ref[:, head:])
-    for copy in fetches:
-        copy.wait()
+    for fetch in fetches:
+        fetch.wait()
     place = lax.broadcasted_iota(jnp.int32, (half, 128), 1)
 
     def build(c, carry):
@@ -121,11 +112,33 @@
                     table[h, pl.ds(start, half), n * 128 : (n + 1) * 128] = jnp.where(valid, value, -1e30)
         return carry
 
-    sizes = [keys * n // 6 for n in (4, 5, 6)]
+    sizes = key_sizes(keys)
     filled = jnp.int32(blocks)
     for used in reversed(sizes[:-1]):
         filled = jnp.where(length <= used, -(-used // width), filled)
     lax.fori_loop(0, filled, build, 0)
+
+
+def attend(length_ref, own_ref, other_ref, table, *refs, heads, scale, slots):
+    weights_hbm, refs = refs[:5], refs[6:]
+    out_ref, weights, sems = refs[:3]
+    keys_of, values_of, queries_of, gates_of, gated_of, scores_of = [refs[n : n + 2] for n in range(3, 15, 2)]
+    later = [pltpu.make_async_copy(w, weights.at[n], sems.at[n]) for n, w in enumerate(weights_hbm)]
+    for copy in later:
+        copy.start()
+    sides = (own_ref, other_ref)
+    blocks, each, width, channels = own_ref.shape
+    head = channels // heads
+    keys, queries = blocks * width, slots * width
+    core, x, z = lax.axis_index("core"), lax.axis_index("x"), lax.axis_index("z_lo")
+    along = lax.axis_size("x")
+    length = length_ref[0]
+    base = (lax.axis_index("y") * lax.axis_size("z_hi") + lax.axis_index("z_hi")) * each
+    bases = [(2 * (z * along + x) + near) * (each * blocks) + base for near in (core, 1 - core)]
+    for ref in values_of:
+        ref[:, head:] = jnp.ones_like(ref[:, head:])
+    for ref in gated_of:
+        ref[...] = jnp.zeros_like(ref)
     for copy in later:
         copy.wait()
     wq, wk, wo = weights[0], weights[1], weights[4]
@@ -135,20 +148,19 @@
     of_head = [(lane >= h * head) & (lane < (h + 1) * head) for h in range(heads)]
 
     def all_rows(used):
-        def cells(n, chosen):
-            side, t = n // each, lax.rem(n, each)
-            return jnp.concatenate([both[side, c, t] for c in chosen], axis=0)
-
-        def project_keys(n, to):
-            keys_of[to][:used] = contract(cells(n, range(-(-used // width)))[:used], wk, 1, 0).astype(bf16)
-
-        def project_values(n, to):
-            value = contract(wv, cells(n, range(-(-used // width)))[:used], 1, 1).astype(bf16)
+        def cells(t, side, chosen):
+            return jnp.concatenate([sides[side][c, t] for c in chosen], axis=0)
+
+        def project_keys(t, to):
+            keys_of[to][:used] = contract(cells(t, to, range(-(-used // width)))[:used], wk, 1, 0).astype(bf16)
+
+        def project_values(t, to):
+            value = contract(wv, cells(t, to, range(-(-used // width)))[:used], 1, 1).astype(bf16)
             for h in range(heads):
                 values_of[to][h, :head, :used] = value[h * head : (h + 1) * head]
 
-        def project_queries(n, to):
-            asked = cells(n, [2 * q + core for q in range(slots)])
+        def project_queries(t, to):
+            asked = cells(t, to, [2 * q + core for q in range(slots)])
             query = (contract(asked, wq, 1, 0) * scale).astype(bf16)
             for h in range(heads):
                 for p in range(slots):
@@ -156,8 +168,8 @@
                     block = query[q * width : (q + 1) * width]
                     queries_of[to][h, p * width : (p + 1) * width] = jnp.where(of_head[h], block, jnp.zeros_like(block))
 
-        def project_gates(n, to):
-            asked = cells(n, [2 * q + core for q in range(slots)])
+        def project_gates(t, to):
+            asked = cells(t, to, [2 * q + core for q in range(slots)])
             gates_of[to][...] = jax.nn.sigmoid(contract(wg, asked, 1, 1)).astype(bf16).astype(f32)
 
         def score(at, h):
@@ -169,8 +181,16 @@
             exponent = jnp.exp(scores_of[h % 2][:used] - highest).astype(bf16)
             return contract(values_of[at][h, :, :used], exponent, 1, 0)
 
-        def one_row(n, at, top):
-            following = jnp.minimum(n + 1, 2 * each - 1)
+        def finish(t, at):
+            update = contract(gated_of[at][...], wo, 0, 0)
+            row_ok = bases[at] + t < length
+            row = lax.broadcasted_iota(jnp.int32, (width, channels), 0)
+            for q in range(slots):
+                ok = (row + (2 * q + core) * width < length) & row_ok
+                piece = update[q * width : (q + 1) * width]
+                out_ref[at, q, t] = jnp.where(ok, piece, 0.0).astype(bf16)
+
+        def one_row(at, before, following, top):
             for h in range(heads):
                 highest = jnp.max(top, 0, keepdims=True)
                 top = score(at, h + 1) if h + 1 < heads else score(1 - at, 0)
@@ -182,25 +202,24 @@
                     project_values(following, 1 - at)
                 if h == 2:
                     project_gates(following, 1 - at)
+                    finish(before, 1 - at)
                 blended = total[:head] / total[head : head + 1]
                 if h > 0:
                     blended = jnp.concatenate([blended[:, h * width :], blended[:, : h * width]], axis=1)
                 part = slice(h * head, (h + 1) * head)
                 gated_of[at][part] = (gates_of[at][part] * blended).astype(bf16)
-            update = contract(gated_of[at][...], wo, 0, 0)
-            side, t = n // each, lax.rem(n, each)
-            row_ok = jnp.where(side == 0, own_base, other_base) + t < length
-            row = lax.broadcasted_iota(jnp.int32, (width, channels), 0)
-            for q in range(slots):
-                ok = (row + (2 * q + core) * width < length) & row_ok
-                piece = update[q * width : (q + 1) * width]
-                out_ref[side, q, t] = jnp.where(ok, piece, 0.0).astype(bf16)
             return top
+
+        def two_rows(t, top):
+            top = one_row(0, jnp.maximum(t - 1, 0), t, top)
+            return one_row(1, t, jnp.minimum(t + 1, each - 1), top)
 
         for first in (project_keys, project_queries, project_values, project_gates):
             first(0, 0)
-        lax.fori_loop(0, each, lambda n, top: one_row(2 * n + 1, 1, one_row(2 * n, 0, top)), score(0, 0))
-
+        lax.fori_loop(0, each, two_rows, score(0, 0))
+        finish(each - 1, 1)
+
+    sizes = key_sizes(keys)
     for n, used in enumerate(sizes):
         fits = length <= used
         if n > 0:
@@ -223,9 +242,9 @@
     heads = w_bias.shape[1]
     half = tile_cols // 2
     lanes = 2 * heads * tile_rows
-    step = 12
+    cuts = [tile_rows * n // 6 for n in (0, 1, 3, 5, 6)]
     return pl.pallas_call(
-        functools.partial(prepare, step=step),
+        functools.partial(prepare, cuts=cuts),
         out_shape=(
             jax.ShapeDtypeStruct(pair.shape, bf16),
             jax.ShapeDtypeStruct((across, half, lanes), bf16),
@@ -234,9 +253,9 @@
         out_specs=(HBM, VMEM),
         scratch_shapes=[
             pltpu.VMEM(pair.shape, bf16),
-            pltpu.SemaphoreType.DMA((tile_rows // step,)),
+            pltpu.SemaphoreType.DMA((len(cuts) - 1,)),
             pltpu.VMEM(pair.shape, bf16),
-            pltpu.SemaphoreType.DMA((tile_rows // step,)),
+            pltpu.SemaphoreType.DMA((len(cuts) - 1,)),
             pltpu.VMEM((1, channels), f32),
             pltpu.VMEM((heads, channels), bf16),
             pltpu.SemaphoreType.DMA((2,)),
@@ -263,24 +282,34 @@
     )(*arrays)
 
 
-def run_attend(length, own, other, parts, weights, passed, heads):
-    blocks, each, width, channels = own.shape
+def run_build(length, parts, heads, width):
     slots = len(parts)
-    keys, queries = blocks * width, slots * width
+    blocks, half, lanes = parts[0].shape
+    return pl.pallas_call(
+        functools.partial(build_table, heads=heads, width=width),
+        out_shape=jax.ShapeDtypeStruct((heads, blocks * width, slots * width), f32),
+        in_specs=[SMEM] + [HBM] * slots,
+        out_specs=VMEM,
+        scratch_shapes=[pltpu.VMEM((slots, blocks, half, lanes), bf16), pltpu.SemaphoreType.DMA((slots,))],
+        compiler_params=pltpu.CompilerParams(vmem_limit_bytes=8 << 20),
+        cost_estimate=pl.CostEstimate(flops=4_000_000, transcendentals=0, bytes_accessed=7_000_000),
+        name="build",
+    )(length, *parts)
+
+
+def run_attend(length, own, other, table, weights, passed):
+    _, each, width, channels = own.shape
+    heads, keys, queries = table.shape
+    slots = queries // width
     head = channels // heads
     return pl.pallas_call(
         functools.partial(attend, heads=heads, scale=head**-0.5, slots=slots),
         out_shape=jax.ShapeDtypeStruct((2, slots, each, width, channels), bf16),
-        in_specs=[SMEM] + [HBM] * (slots + 8),
+        in_specs=[SMEM] + [VMEM] * 3 + [HBM] * 6,
         out_specs=VMEM,
         scratch_shapes=[
             pltpu.VMEM((5, channels, channels), bf16),
             pltpu.SemaphoreType.DMA((5,)),
-            pltpu.VMEM((slots, *parts[0].shape), bf16),
-            pltpu.SemaphoreType.DMA((slots,)),
-            pltpu.VMEM((2, *own.shape), bf16),
-            pltpu.SemaphoreType.DMA((2,)),
-            pltpu.VMEM((heads, keys, queries), f32),
         ]
         + [pltpu.VMEM((keys, channels), bf16)] * 2
         + [pltpu.VMEM((heads, head + 16, keys), bf16)] * 2
@@ -288,10 +317,10 @@
         + [pltpu.VMEM((channels, queries), f32)] * 2
         + [pltpu.VMEM((channels, queries), bf16)] * 2
         + [pltpu.VMEM((keys, queries), f32)] * 2,
-        compiler_params=pltpu.CompilerParams(vmem_limit_bytes=24 << 20),
+        compiler_params=pltpu.CompilerParams(vmem_limit_bytes=20 << 20),
         cost_estimate=pl.CostEstimate(flops=2_500_000_000, transcendentals=7_000_000, bytes_accessed=4_000_000),
         name="attend",
-    )(length, own, other, *parts, *weights, passed)
+    )(length, own, other, table, *weights, passed)
 
 
 def shifted(value, axis, by):
@@ -318,7 +347,8 @@
     passed = run_gate([right, below_left, far, below_far])
     other = shifted(own, "core", 1)
     parts = [mine, left, right, below, far, below_left, below_right, below_far]
-    out = run_attend(valid_length, own, other, parts, weights, passed, heads)
+    table = run_build(valid_length, parts, heads, tile_cols)
+    out = run_attend(valid_length, own, other, table, weights, passed)
     theirs = shifted(out[1], "core", 1)
     core = lax.axis_index("core")
     even = jnp.where(core == 0, out[0], theirs)

time: 120 us -> 120 us (level)
    pallas_call x1, Pallas kernels: 13.5 us -> 10.8 us  [run_attend(): pl.pallas_call(functools.partial(attend, heads=heads, scale=head ** (-0.5...]
    pallas_call x1 -> x2, Pallas kernels: 4.08 us -> 6.45 us  [the longest x1 4.05 us: run_prepare(): pl.pallas_call(functools.partial(prepare, cuts=cuts), out_shape=(jax.Shap...]
  transfers between devices with their start and end apart: 10 -> 10, of which waited for: 7 -> 7; matrix products, arithmetic and copies ran while one was open for 0% -> 0% of each run, Pallas kernels for 0% -> 2%
where the time goes in v6:
time: 120 us; the launch traced here: 118 us
  blocking collectives  54.6 us (46%)
  waiting for transfers between devices  33.3 us (28%)
  Pallas kernels  17.2 us (14%)
  starting transfers between devices  11.2 us (9%)
    ppermute x9, waiting for transfers between devices, shifted(): return lax.ppermute(value, axis, [(k, (k + by) % n) for k in range(n)])  32.7 us
    all_to_all x1, blocking collectives, per_device_inner(): return lax.all_to_all(update, COL, 0, 0, tiled=True)  29.6 us
    all_to_all x1, blocking collectives, per_device_inner(): mine = lax.all_to_all(bias, COL, 0, 0, tiled=True)  25 us
    pallas_call x1, Pallas kernels, run_attend(): pl.pallas_call(functools.partial(attend, heads=heads, scale=head ** (-0.5...  10.8 us
    ppermute x9, starting transfers between devices, shifted(): return lax.ppermute(value, axis, [(k, (k + by) % n) for k in range(n)])  7.61 us
    pallas_call x1, Pallas kernels, run_prepare(): pl.pallas_call(functools.partial(prepare, cuts=cuts), out_shape=(jax.Shap...  4.05 us
    all_to_all x1, starting transfers between devices, per_device_inner(): lax.all_to_all(normed.reshape(across, each, tile_cols, channels), COL, 0,...  3.58 us
  transfers between devices with their start and end apart: 10, of which 7 were waited for; matrix products, arithmetic and copies ran while one was open for 0% of the time, Pallas kernels for 2%

profile of v6, /device:TPU:2, one launch (start us, length us, event | category | flops | bytes accessed | tf_op | source)
XLA Modules:
  0.0 118.0 jit_solution(11198742413248728844)
XLA Ops:
  0.0 4.1 %prepare.1 = (bf16[48,48,128]{2,1,0:T(8,128)(2,1)}, bf16[16,24,384]{2,1,0:T(8,128)(2,1)S(1)}) custom-call(bf16[48,48,128]{2,1,0:T(8,128)(2,1)} %pair_hbm.1, f32[1,128]{1,0:T(1,128)} %bitcast.18, bf16[4,128]{1,0:T(4,128)(2,1)} %bitcast.17), custom_call_target="tpu_custom_call" | custom-call | tf_op jit(solution)/shard_map/prepare/pallas_call | solution.py:246
  4.1 25.0 %all_to_all.15.refs_0_ = bf16[16,24,384]{2,1,0:T(8,128)(2,1)S(1)} all-to-all(bf16[16,24,384]{2,1,0:T(8,128)(2,1)S(1)} %get-tuple-element.8), channel_id=1, replica_groups=mesh['z_lo'=2,'x'=4,'core'=2,'y'=4,'z_hi'=4] {'y','z_hi'}, dimensions={0} | all-to-all | bytes 589824 | tf_op jit(solution)/shard_map/all_to_all | solution.py:338
  29.0 3.6 %all-to-all-start = ((bf16[16,3,48,128]{3,2,1,0:T(8,128)(2,1)}), bf16[16,3,48,128]{3,2,1,0:T(8,128)(2,1)S(1)}, u32[]{:S(2)}, u32[]{:S(2)}) async-start(bf16[16,3,48,128]{3,2,1,0:T(8,128)(2,1)} %bitcast.2), calls=%async_computation | async-start | bytes 1179648 | tf_op jit(solution)/shard_map/all_to_all | solution.py:339
  32.6 1.1 collective-permute-start.3
  33.7 1.5 %collective-permute-start.1 = (bf16[16,24,384]{2,1,0:T(8,128)(2,1)S(1)}, bf16[16,24,384]{2,1,0:T(8,128)(2,1)S(1)}, u32[]{:S(2)}, u32[]{:S(2)}) collective-permute-start(bf16[16,24,384]{2,1,0:T(8,128)(2,1)S(1)} %all_to_all.15.refs_0_), channel_id=1, source_target_pairs={{0,32},{32,64},{64,96},{96,0},{1,33},{33,65},{65,97},{97,1},{2,34}... | collective-permute-start | bytes 884744 | tf_op jit(solution)/shard_map/ppermute | solution.py:328
  35.2 17.0 %collective-permute-done.3.refs_3_ = bf16[16,24,384]{2,1,0:T(8,128)(2,1)S(1)} collective-permute-done((bf16[16,24,384]{2,1,0:T(8,128)(2,1)S(1)}, bf16[16,24,384]{2,1,0:T(8,128)(2,1)S(1)}, u32[]{:S(2)}, u32[]{:S(2)}) %collective-permute-start.3) | collective-permute-done | bytes 294944 | tf_op jit(solution)/shard_map/ppermute | solution.py:328
  52.2 0.6 collective-permute-start.6
  52.8 0.6 all-to-all-done.own_ref
  53.3 0.0 collective-permute-start
  53.3 2.2 %collective-permute-start.2 = (bf16[16,24,384]{2,1,0:T(8,128)(2,1)S(1)}, bf16[16,24,384]{2,1,0:T(8,128)(2,1)S(1)}, u32[]{:S(2)}, u32[]{:S(2)}) collective-permute-start(bf16[16,24,384]{2,1,0:T(8,128)(2,1)S(1)} %all_to_all.15.refs_0_), channel_id=1, source_target_pairs={{0,96},{32,0},{64,32},{96,64},{1,97},{33,1},{65,33},{97,65},{2,98}... | collective-permute-start | bytes 884744 | tf_op jit(solution)/shard_map/ppermute | solution.py:328
  55.5 0.0 collective-permute-start.5
  55.5 0.0 collective-permute-done.1.refs_1_
  55.5 1.4 %collective-permute-start.4 = (bf16[16,24,384]{2,1,0:T(8,128)(2,1)S(1)}, bf16[16,24,384]{2,1,0:T(8,128)(2,1)S(1)}, u32[]{:S(2)}, u32[]{:S(2)}) collective-permute-start(bf16[16,24,384]{2,1,0:T(8,128)(2,1)S(1)} %collective-permute-done.1.refs_1_), channel_id=1, source_target_pairs={{0,32},{32,64},{64,96},{96,0},{1,33},{33,65},{65,97},{97,1},{2,34}... | collective-permute-start | bytes 884744 | tf_op jit(solution)/shard_map/ppermute | solution.py:328
  56.9 5.2 %collective-permute-done.6.refs_6_ = bf16[16,24,384]{2,1,0:T(8,128)(2,1)S(1)} collective-permute-done((bf16[16,24,384]{2,1,0:T(8,128)(2,1)S(1)}, bf16[16,24,384]{2,1,0:T(8,128)(2,1)S(1)}, u32[]{:S(2)}, u32[]{:S(2)}) %collective-permute-start.6) | collective-permute-done | bytes 294944 | tf_op jit(solution)/shard_map/ppermute | solution.py:328
  62.1 0.8 collective-permute-start.7
  63.6 4.8 %collective-permute-done.2.refs_2_.refs_0_ = bf16[16,24,384]{2,1,0:T(8,128)(2,1)S(1)} collective-permute-done((bf16[16,24,384]{2,1,0:T(8,128)(2,1)S(1)}, bf16[16,24,384]{2,1,0:T(8,128)(2,1)S(1)}, u32[]{:S(2)}, u32[]{:S(2)}) %collective-permute-start.2) | collective-permute-done | bytes 294944 | tf_op jit(solution)/shard_map/ppermute | solution.py:328
  68.4 0.0 collective-permute-done.5.refs_5_.refs_1_
  68.4 2.6 %collective-permute-done.4.refs_4_.refs_2_ = bf16[16,24,384]{2,1,0:T(8,128)(2,1)S(1)} collective-permute-done((bf16[16,24,384]{2,1,0:T(8,128)(2,1)S(1)}, bf16[16,24,384]{2,1,0:T(8,128)(2,1)S(1)}, u32[]{:S(2)}, u32[]{:S(2)}) %collective-permute-start.4) | collective-permute-done | bytes 294944 | tf_op jit(solution)/shard_map/ppermute | solution.py:328
  71.0 1.5 %collective-permute-done.7.refs_7_.refs_3_ = bf16[16,24,384]{2,1,0:T(8,128)(2,1)S(1)} collective-permute-done((bf16[16,24,384]{2,1,0:T(8,128)(2,1)S(1)}, bf16[16,24,384]{2,1,0:T(8,128)(2,1)S(1)}, u32[]{:S(2)}, u32[]{:S(2)}) %collective-permute-start.7) | collective-permute-done | bytes 294944 | tf_op jit(solution)/shard_map/ppermute | solution.py:328
  72.5 2.4 %build.1.table = f32[4,768,384]{2,1,0:T(8,128)S(1)} custom-call(s32[1]{0:T(128)S(6)} %copy.12.length_ref, bf16[16,24,384]{2,1,0:T(8,128)(2,1)S(1)} %all_to_all.15.refs_0_, bf16[16,24,384]{2,1,0:T(8,128)(2,1)S(1)} %collective-permute-done.1.refs_1_, bf16[16,24,384]{2,1,0:T(8,128)(2,1)S(1)} %collective-permute-done.2.refs_2_.refs_0_, ...), custom_call_target="tpu_custom_call" | custom-call | flops 4000000 | bytes 7000000 | tf_op jit(solution)/shard_map/build/pallas_call | solution.py:288
  74.9 0.0 collective-permute-done.other_ref
  74.9 10.8 %attend.1 = bf16[2,8,3,48,128]{4,3,2,1,0:T(8,128)(2,1)S(1)} custom-call(s32[1]{0:T(128)S(6)} %copy.12.length_ref, bf16[16,3,48,128]{3,2,1,0:T(8,128)(2,1)S(1)} %all-to-all-done.own_ref, bf16[16,3,48,128]{3,2,1,0:T(8,128)(2,1)S(1)} %collective-permute-done.other_ref, f32[4,768,384]{2,1,0:T(8,128)S(1)} %build.1.table, bf16[128,128]{1,0:T(8,128)(2,1)} %refs_0_.1, ...), custom_call_target="tpu_custom_call" | custom-call | flops 2500000000 | bytes 4000000 | tf_op jit(solution)/shard_map/attend/pallas_call | solution.py:305
  85.7 0.1 collective-permute-start.8
  85.8 1.6 %collective-permute-done.8 = bf16[8,3,48,128]{3,2,1,0:T(8,128)(2,1)S(1)} collective-permute-done((bf16[8,3,48,128]{3,2,1,0:T(8,128)(2,1)S(1)}, bf16[8,3,48,128]{3,2,1,0:T(8,128)(2,1)S(1)}, u32[]{:S(2)}, u32[]{:S(2)}) %collective-permute-start.8) | collective-permute-done | bytes 294944 | tf_op jit(solution)/shard_map/ppermute | solution.py:328
  87.4 0.1 pad_maximum_fusion
  87.6 29.6 %all_to_all.16 = bf16[48,48,128]{2,1,0:T(8,128)(2,1)S(1)} all-to-all(bf16[48,48,128]{2,1,0:T(8,128)(2,1)S(1)} %bitcast.16), channel_id=1, replica_groups=mesh['z_lo'=2,'x'=4,'core'=2,'y'=4,'z_hi'=4] {'y','z_hi'}, dimensions={0} | all-to-all | bytes 1179648 | tf_op jit(solution)/shard_map/all_to_all | solution.py:357
  117.2 0.8 copy.13
  (4 shorter events, 0.1 us)
Async XLA Ops:
  29.0 24.3 %all-to-all-start = ((bf16[16,3,48,128]{3,2,1,0:T(8,128)(2,1)}), bf16[16,3,48,128]{3,2,1,0:T(8,128)(2,1)S(1)}, u32[]{:S(2)}, u32[]{:S(2)}) async-start(bf16[16,3,48,128]{3,2,1,0:T(8,128)(2,1)} %bitcast.2), calls=%async_computation | async-start | bytes 1179648 | tf_op jit(solution)/shard_map/all_to_all | solution.py:339
  32.6 19.6 %collective-permute-start.3 = (bf16[16,24,384]{2,1,0:T(8,128)(2,1)S(1)}, bf16[16,24,384]{2,1,0:T(8,128)(2,1)S(1)}, u32[]{:S(2)}, u32[]{:S(2)}) collective-permute-start(bf16[16,24,384]{2,1,0:T(8,128)(2,1)S(1)} %all_to_all.15.refs_0_), channel_id=1, source_target_pairs={{0,128},{128,0},{1,129},{129,1},{2,130},{130,2},{3,131},{131,3},{4... | collective-permute-start | bytes 884744 | tf_op jit(solution)/shard_map/ppermute | solution.py:328
  33.7 21.8 %collective-permute-start.1 = (bf16[16,24,384]{2,1,0:T(8,128)(2,1)S(1)}, bf16[16,24,384]{2,1,0:T(8,128)(2,1)S(1)}, u32[]{:S(2)}, u32[]{:S(2)}) collective-permute-start(bf16[16,24,384]{2,1,0:T(8,128)(2,1)S(1)} %all_to_all.15.refs_0_), channel_id=1, source_target_pairs={{0,32},{32,64},{64,96},{96,0},{1,33},{33,65},{65,97},{97,1},{2,34}... | collective-permute-start | bytes 884744 | tf_op jit(solution)/shard_map/ppermute | solution.py:328
  52.2 9.9 %collective-permute-start.6 = (bf16[16,24,384]{2,1,0:T(8,128)(2,1)S(1)}, bf16[16,24,384]{2,1,0:T(8,128)(2,1)S(1)}, u32[]{:S(2)}, u32[]{:S(2)}) collective-permute-start(bf16[16,24,384]{2,1,0:T(8,128)(2,1)S(1)} %collective-permute-done.3.refs_3_), channel_id=1, source_target_pairs={{0,96},{32,0},{64,32},{96,64},{1,97},{33,1},{65,33},{97,65},{2,98}... | collective-permute-start | bytes 884744 | tf_op jit(solution)/shard_map/ppermute | solution.py:328
  53.3 21.6 %collective-permute-start = (bf16[16,3,48,128]{3,2,1,0:T(8,128)(2,1)S(1)}, bf16[16,3,48,128]{3,2,1,0:T(8,128)(2,1)S(1)}, u32[]{:S(2)}, u32[]{:S(2)}) collective-permute-start(bf16[16,3,48,128]{3,2,1,0:T(8,128)(2,1)S(1)} %all-to-all-done.own_ref), channel_id=1, source_target_pairs={{0,16},{16,0},{1,17},{17,1},{2,18},{18,2},{3,19},{19,3},{4,20},{20... | collective-permute-start | bytes 1769480 | tf_op jit(solution)/shard_map/ppermute | solution.py:328
  53.3 15.1 %collective-permute-start.2 = (bf16[16,24,384]{2,1,0:T(8,128)(2,1)S(1)}, bf16[16,24,384]{2,1,0:T(8,128)(2,1)S(1)}, u32[]{:S(2)}, u32[]{:S(2)}) collective-permute-start(bf16[16,24,384]{2,1,0:T(8,128)(2,1)S(1)} %all_to_all.15.refs_0_), channel_id=1, source_target_pairs={{0,96},{32,0},{64,32},{96,64},{1,97},{33,1},{65,33},{97,65},{2,98}... | collective-permute-start | bytes 884744 | tf_op jit(solution)/shard_map/ppermute | solution.py:328
  55.5 12.9 %collective-permute-start.5 = (bf16[16,24,384]{2,1,0:T(8,128)(2,1)S(1)}, bf16[16,24,384]{2,1,0:T(8,128)(2,1)S(1)}, u32[]{:S(2)}, u32[]{:S(2)}) collective-permute-start(bf16[16,24,384]{2,1,0:T(8,128)(2,1)S(1)} %collective-permute-done.3.refs_3_), channel_id=1, source_target_pairs={{0,32},{32,64},{64,96},{96,0},{1,33},{33,65},{65,97},{97,1},{2,34}... | collective-permute-start | bytes 884744 | tf_op jit(solution)/shard_map/ppermute | solution.py:328
  55.5 15.5 %collective-permute-start.4 = (bf16[16,24,384]{2,1,0:T(8,128)(2,1)S(1)}, bf16[16,24,384]{2,1,0:T(8,128)(2,1)S(1)}, u32[]{:S(2)}, u32[]{:S(2)}) collective-permute-start(bf16[16,24,384]{2,1,0:T(8,128)(2,1)S(1)} %collective-permute-done.1.refs_1_), channel_id=1, source_target_pairs={{0,32},{32,64},{64,96},{96,0},{1,33},{33,65},{65,97},{97,1},{2,34}... | collective-permute-start | bytes 884744 | tf_op jit(solution)/shard_map/ppermute | solution.py:328
  62.1 10.4 %collective-permute-start.7 = (bf16[16,24,384]{2,1,0:T(8,128)(2,1)S(1)}, bf16[16,24,384]{2,1,0:T(8,128)(2,1)S(1)}, u32[]{:S(2)}, u32[]{:S(2)}) collective-permute-start(bf16[16,24,384]{2,1,0:T(8,128)(2,1)S(1)} %collective-permute-done.6.refs_6_), channel_id=1, source_target_pairs={{0,96},{32,0},{64,32},{96,64},{1,97},{33,1},{65,33},{97,65},{2,98}... | collective-permute-start | bytes 884744 | tf_op jit(solution)/shard_map/ppermute | solution.py:328
  85.7 1.7 %collective-permute-start.8 = (bf16[8,3,48,128]{3,2,1,0:T(8,128)(2,1)S(1)}, bf16[8,3,48,128]{3,2,1,0:T(8,128)(2,1)S(1)}, u32[]{:S(2)}, u32[]{:S(2)}) collective-permute-start(bf16[8,3,48,128]{3,2,1,0:T(8,128)(2,1)S(1)} %slice_bitcast_fusion), channel_id=1, source_target_pairs={{0,16},{16,0},{1,17},{17,1},{2,18},{18,2},{3,19},{19,3},{4,20},{20... | collective-permute-start | bytes 884744 | tf_op jit(solution)/shard_map/ppermute | solution.py:328
